TPU v7x, 128 devices: a whole 4x4x4 slice. The times are simulated.
128 devices in a mesh: samp: 4 (over x), var: 32 (over z, y, core).
Axes of the slice: x: 4, y: 4, z: 4, core: 2. Of those that a mesh axis runs over, the one named last changes fastest.
Arguments:
- genotypes: float32 [4096, 65536], P('samp', 'var'), may hold values from 0 to 2
- phenotype: float32 [4096], P('samp'), may hold values from -6 to 6
- win_start: int32 [65536], P('var'), may hold values from 0 to 65535, as said below
- win_end: int32 [65536], P('var'), may hold values from 1 to 65536, as said below
Outputs:
- effects: float32 [65536], P('var')
- ld_scores: float32 [65536], P('var')
Inputs may be any that keep to these rules, and one draw needn't show every extreme that they name: win_start[j] <= j < win_end[j], j - win_start[j] <= 512 and win_end[j] - j <= 513, both reached with equality by some variant; k lies in the window of j exactly when j lies in the window of k; win_start and win_end never fall along the variants. `win_end`: see win_start.
All inputs are finite; a program needn't handle non-finite values.
Results may differ from a plain program's by a relative error of at most 0.0003.
Values sent between devices are 32-bit elements; how exact they have to be, the bound alone decides.
A program may use at most 256 MiB of HBM per device.

v0:
```python
import math

import jax
import jax.numpy as jnp
from jax import lax
from jax.sharding import PartitionSpec as P

HALF_BAND = 512
BLOCK = 128
ITERS = 3


EPS = 1e-05
SHRINK = 1.5
HIGH = lax.Precision.HIGHEST


def padded(cells, sides, width):
    for axis, dim in sides:
        count = lax.axis_size(axis)
        ends = count - 1
        head = lax.slice_in_dim(cells, 0, width, axis=dim)
        tail = lax.slice_in_dim(cells, cells.shape[dim] - width, cells.shape[dim], axis=dim)
        cells = jnp.concatenate(
            [
                lax.ppermute(tail, axis, [(i, (i + 1) % count) for i in range(ends)]),
                cells,
                lax.ppermute(head, axis, [((i + 1) % count, i) for i in range(ends)]),
            ],
            axis=dim,
        )
    return cells


def gram_blocks(scaled, extended, blocks, span):

    def one_block(index):
        begin = index * BLOCK
        rows = lax.dynamic_slice_in_dim(scaled, begin, BLOCK, 1)
        near = lax.dynamic_slice_in_dim(extended, begin, span, 1)
        return lax.dot_general(
            rows, near, (((0,), (0,)), ((), ())), precision=HIGH, preferred_element_type=jnp.float32
        )

    return lax.map(one_block, jnp.arange(blocks, dtype=jnp.int32))


def shards(genotypes, phenotype, win_start, win_end):
    local_rows, width = genotypes.shape
    count = local_rows * lax.axis_size("samp")
    mean = lax.psum(jnp.sum(genotypes, axis=0), "samp") / count
    centered = genotypes - mean
    spread = lax.psum(jnp.sum(centered * centered, axis=0), "samp") / count
    scaled = centered * lax.rsqrt(spread + EPS)
    extended = padded(scaled, (("var", 1),), HALF_BAND)
    span = BLOCK + 2 * HALF_BAND
    lead = HALF_BAND
    local_marginal = jnp.dot(phenotype, scaled, precision=HIGH, preferred_element_type=jnp.float32)
    blocks = width // BLOCK
    partial_value = gram_blocks(scaled, extended, blocks, span)
    band_sum, marginal_sum = lax.psum((partial_value, local_marginal), "samp")
    offset = lax.axis_index("var") * width
    firsts = jnp.arange(blocks, dtype=jnp.int32) * BLOCK
    column = (
        offset + firsts[:, None, None] - lead + jnp.arange(span, dtype=jnp.int32)[None, None, :]
    )
    lows = win_start.reshape(blocks, BLOCK)[:, :, None]
    highs = win_end.reshape(blocks, BLOCK)[:, :, None]
    inside = (column >= lows) & (column < highs)
    band = jnp.where(inside, band_sum / count, jnp.float32(0.0))
    score_part = jnp.sum(band * band, axis=2).reshape(blocks * BLOCK)
    picks = firsts[:, None] + jnp.arange(span, dtype=jnp.int32)[None, :]

    def squares_of(residual):
        return lax.psum(jnp.sum(residual * residual), "var")

    marginal = marginal_sum / math.sqrt(count)
    effects = jnp.zeros((width,), jnp.float32)
    residual = marginal
    direction = marginal
    norm_now = squares_of(residual)
    for step in range(ITERS):
        wide = padded(direction, (("var", 0),), HALF_BAND)
        windows = wide[picks]
        product = jnp.einsum("bij,bj->bi", band, windows, precision=HIGH).reshape(blocks * BLOCK)
        image = product + SHRINK * direction
        alpha = norm_now / lax.psum(jnp.sum(direction * image), "var")
        effects = effects + alpha * direction
        residual = residual - alpha * image
        norm_next = squares_of(residual)
        direction = residual + norm_next / norm_now * direction
        norm_now = norm_next
    return (effects, score_part)


def solution(mesh):
    in_specs = (P("samp", "var"), P("samp"), P("var"), P("var"))
    out_specs = (P("var"), P("var"))
    return jax.shard_map(shards, mesh=mesh, in_specs=in_specs, out_specs=out_specs, check_vma=False)
```

profile of v0, /device:TPU:0, one launch (start us, length us, event | category | flops | bytes accessed | tf_op | source)
XLA Modules:
  0.0 979.1 jit_solution(14776190162422267295)
XLA Ops:
  11.0 10.7 %psum.70 = f32[2048]{0:T(1024)S(1)} all-reduce(f32[2048]{0:T(1024)S(1)} %reduce_sum.81), channel_id=1, replica_groups=mesh['samp'=4,'var'=32] {'samp'}, use_global_device_ids=true, to_apply=%region_1.0 | all-reduce | flops 2048 | bytes 16384 | tf_op jit(solution)/shard_map/psum | solution.py:51
  26.0 7.8 psum.71
  53.5 9.3 pad_maximum_fusion
  62.8 117.9 %while.11 = (s32[]{:T(128)}, f32[16,128,1152]{2,1,0:T(8,128)}, s32[16]{0:T(128)S(1)}, f32[1024,2048]{1,0:T(8,128)}, f32[1024,3072]{1,0:T(8,128)}, /*index=5*/s32[1]{0:T(128)}) while((s32[]{:T(128)}, f32[16,128,1152]{2,1,0:T(8,128)}, s32[16]{0:T(128)S(1)}, f32[1024,2048]{1,0:T(8,128)}, f32[1024,3072]{1,0:T(8,128)}, ...), condition=%wide.region_8.9_spmd.clone, body=%wide.region_7.8_spmd.sunk.clone | while | flops 1811939328 | bytes 5833376 | solution.py:45
  64.1 6.1 fusion.37
  71.5 6.2 fusion.37
  78.9 6.1 fusion.37
  86.2 6.1 fusion.37
  93.6 6.1 fusion.37
  101.0 6.1 fusion.37
  108.3 6.1 fusion.37
  115.7 6.1 fusion.37
  130.4 6.1 fusion.37
  145.2 6.1 fusion.37
  152.5 6.1 fusion.37
  159.9 6.1 fusion.37
  174.6 6.1 fusion.37
  180.8 6.7 fusion.23
  187.5 9.9 %psum.72 = f32[2048]{0:T(1024)S(1)} all-reduce(f32[2048]{0:T(1024)S(1)} %bitcast.45), channel_id=1, replica_groups=mesh['samp'=4,'var'=32] {'samp'}, use_global_device_ids=true, to_apply=%region_4.5 | all-reduce | flops 2048 | bytes 16384 | tf_op jit(solution)/shard_map/psum | solution.py:61
  197.4 22.1 %collective-permute-start.2 = (f32[512]{0:T(512)S(1)}, f32[512]{0:T(512)S(1)}, u32[]{:S(2)}, u32[]{:S(2)}) collective-permute-start(f32[512]{0:T(512)S(1)} %get-tuple-element.52), channel_id=1, source_target_pairs={{0,1},{1,2},{2,3},{3,4},{4,5},{5,6},{6,7},{7,8},{8,9},{9,10},{10,1... | collective-permute-start | bytes 6152 | tf_op jit(solution)/shard_map/ppermute | solution.py:26
  223.6 101.8 %gather_fusion = f32[18432]{0:T(1024)S(1)} fusion(f32[3072]{0:T(1024)S(1)} %pad_maximum_fusion.1, s32[18432]{0:T(1024)S(1)} %broadcast_clamp_fusion), kind=kCustom, calls=%fused_computation | custom fusion | bytes 221184 | tf_op jit(solution)/shard_map/gather | solution.py:84
  325.4 56.9 %all-reduce.3.cloned.1.call-done = f32[16,128,1152]{2,1,0:T(8,128)} async-done(((f32[16,128,1152]{2,1,0:T(8,128)}), f32[16,128,1152]{2,1,0:T(8,128)}) %all-reduce.3.cloned.1.call-update) | async-done | bytes 9437200 | tf_op jit(solution)/shard_map/psum | solution.py:61
  382.3 12.7 %fusion.12 = f32[16,1,128]{2,1,0:T(1,128)S(1)} fusion(f32[16,1152,1]{1,2,0:T(1,128)S(1)} %bitcast.39, f32[16,128,1152]{2,1,0:T(8,128)} %all-reduce.3.cloned.1.call-done, s32[16,128]{1,0:T(8,128)S(1)} %bitcast.48, s32[16,128]{1,0:T(8,128)S(1)} %bitcast.52, s32[16,1152]{1,0:T(8,128)S(1)} %iota_add_fusion), kind=kOutput, calls=%fused_computation.16 | convolution fusion | flops 40108032 | bytes 9609216 | tf_op jit(solution)/shard_map/bij,bj->bi/dot_general | solution.py:85
  395.6 67.9 %all-reduce = (f32[]{:T(128)}, f32[]{:T(128)}) all-reduce(f32[]{:T(128)} %get-tuple-element.31, f32[]{:T(128)} %get-tuple-element.30), channel_id=1, replica_groups=mesh['samp'=4,'var'=32] {'var'}, use_global_device_ids=true, to_apply=%region_6.7 | all-reduce | flops 2 | bytes 16 | tf_op jit(solution)/shard_map/psum | solution.py:75
  465.4 63.3 %psum.76 = f32[]{:T(128)} all-reduce(f32[]{:T(128)} %get-tuple-element.44), channel_id=1, replica_groups=mesh['samp'=4,'var'=32] {'var'}, use_global_device_ids=true, to_apply=%region_13.14 | all-reduce | flops 1 | bytes 8 | tf_op jit(solution)/shard_map/psum | solution.py:75
  534.9 101.8 %gather_fusion.1 = f32[18432]{0:T(1024)S(1)} fusion(f32[3072]{0:T(1024)S(1)} %pad_maximum_fusion.2, s32[18432]{0:T(1024)S(1)} %broadcast_clamp_fusion), kind=kCustom, calls=%fused_computation.1 | custom fusion | bytes 221184 | tf_op jit(solution)/shard_map/gather | solution.py:84
  636.6 12.7 %fusion.11 = f32[16,1,128]{2,1,0:T(1,128)S(1)} fusion(f32[16,1152,1]{1,2,0:T(1,128)S(1)} %bitcast.41, f32[16,128,1152]{2,1,0:T(8,128)} %all-reduce.3.cloned.1.call-done, s32[16,128]{1,0:T(8,128)S(1)} %bitcast.49, s32[16,128]{1,0:T(8,128)S(1)} %bitcast.53, s32[16,1152]{1,0:T(8,128)S(1)} %iota_add_fusion), kind=kOutput, calls=%fused_computation.15 | convolution fusion | flops 40108032 | bytes 9609216 | tf_op jit(solution)/shard_map/bij,bj->bi/dot_general | solution.py:85
  650.0 65.2 %psum.77 = f32[]{:T(128)} all-reduce(f32[]{:T(128)} %multiply_reduce_fusion.4), channel_id=1, replica_groups=mesh['samp'=4,'var'=32] {'var'}, use_global_device_ids=true, to_apply=%region_15.16 | all-reduce | flops 1 | bytes 8 | tf_op jit(solution)/shard_map/psum | solution.py:87
  717.1 63.3 %psum.78 = f32[]{:T(128)} all-reduce(f32[]{:T(128)} %multiply_reduce_fusion.3), channel_id=1, replica_groups=mesh['samp'=4,'var'=32] {'var'}, use_global_device_ids=true, to_apply=%region_17.18 | all-reduce | flops 1 | bytes 8 | tf_op jit(solution)/shard_map/psum | solution.py:75
  790.7 101.8 %gather_fusion.2 = f32[18432]{0:T(1024)S(1)} fusion(f32[3072]{0:T(1024)S(1)} %pad_maximum_fusion.3, s32[18432]{0:T(1024)S(1)} %broadcast_clamp_fusion), kind=kCustom, calls=%fused_computation.2 | custom fusion | bytes 221184 | tf_op jit(solution)/shard_map/gather | solution.py:84
  892.5 12.7 %fusion.10 = f32[16,1,128]{2,1,0:T(1,128)S(1)} fusion(f32[16,1152,1]{1,2,0:T(1,128)S(1)} %bitcast.40, f32[16,128,1152]{2,1,0:T(8,128)} %all-reduce.3.cloned.1.call-done, s32[16,128]{1,0:T(8,128)S(1)} %bitcast.51, s32[16,128]{1,0:T(8,128)S(1)} %bitcast.55, s32[16,1152]{1,0:T(8,128)S(1)} %iota_add_fusion), kind=kOutput, calls=%fused_computation.14 | convolution fusion | flops 40108032 | bytes 9609216 | tf_op jit(solution)/shard_map/bij,bj->bi/dot_general | solution.py:85
  905.9 64.4 %psum.79 = f32[]{:T(128)} all-reduce(f32[]{:T(128)} %multiply_reduce_fusion.2), channel_id=1, replica_groups=mesh['samp'=4,'var'=32] {'var'}, use_global_device_ids=true, to_apply=%region_19.20 | all-reduce | flops 1 | bytes 8 | tf_op jit(solution)/shard_map/psum | solution.py:87
  (74 shorter events, 77.1 us)
Async XLA Ops:
  7.2 173.6 %copy-start = (f32[1024]{0:T(1024)S(1)}, f32[1024]{0:T(1024)}, u32[]{:S(2)}) copy-start(f32[1024]{0:T(1024)} %param.7) | copy-start | bytes 12292
  7.2 375.1 %all-reduce.3.cloned.1.call-start = ((), (), s32[]{:S(2)}) async-start(), calls=%async_computation | async-start | bytes 18874368 | tf_op jit(solution)/shard_map/psum | solution.py:61
  38.3 3.3 copy-start.1
  44.0 5.3 collective-permute-start
  45.4 8.1 collective-permute-start.1
  197.4 23.8 %collective-permute-start.2 = (f32[512]{0:T(512)S(1)}, f32[512]{0:T(512)S(1)}, u32[]{:S(2)}, u32[]{:S(2)}) collective-permute-start(f32[512]{0:T(512)S(1)} %get-tuple-element.52), channel_id=1, source_target_pairs={{0,1},{1,2},{2,3},{3,4},{4,5},{5,6},{6,7},{7,8},{8,9},{9,10},{10,1... | collective-permute-start | bytes 6152 | tf_op jit(solution)/shard_map/ppermute | solution.py:26
  219.5 4.1 collective-permute-start.3
  223.6 158.7 %copy-start.2 = (s32[2048]{0:T(1024)S(1)}, s32[2048]{0:T(1024)}, u32[]{:S(2)}) copy-start(s32[2048]{0:T(1024)} %param.9) | copy-start | bytes 24580
  223.6 158.7 %copy-start.3 = (s32[2048]{0:T(1024)S(1)}, s32[2048]{0:T(1024)}, u32[]{:S(2)}) copy-start(s32[2048]{0:T(1024)} %param.8) | copy-start | bytes 24580
  530.0 3.1 collective-permute-start.4
  531.8 3.1 collective-permute-start.5
  781.7 9.0 collective-permute-start.6
  783.5 7.2 collective-permute-start.7
Sparse Core Ops, SparseCore 0:
  180.9 201.3 all-reduce.2
where the time goes:
time: 980 us; the launch traced here: 979 us
  blocking collectives  352 us (36%)
  local copies, waits for them, and re-layouts  320 us (33%)
  matrix products  143 us (15%)
  waiting for transfers between devices  67.8 us (7%)
  starting transfers between devices  32.6 us (3%)
  other arithmetic  31.5 us (3%)
  between operations  21.1 us (2%)
  loops' own time  10.6 us (1%)
    gather x3, local copies, waits for them, and re-layouts, shards(): windows = wide[picks]  305 us
    psum x3, blocking collectives, squares_of(): return lax.psum(jnp.sum(residual * residual), 'var')  194 us
    psum x2, blocking collectives, shards(): alpha = norm_now / lax.psum(jnp.sum(direction * image), 'var')  130 us
    dot_general x16, matrix products, one_block(): lax.dot_general(rows, near, (((0,), (0,)), ((), ())), precision=HIGH, pre...  98 us
    psum x1, waiting for transfers between devices, shards(): band_sum, marginal_sum = lax.psum((partial_value, local_marginal), 'samp')  56.9 us
    dot_general x3, matrix products, shards(): jnp.einsum('bij,bj->bi', band, windows, precision=HIGH)  38.1 us
    ppermute x4, starting transfers between devices, padded(): lax.ppermute(tail, axis, [(i, (i + 1) % count) for i in range(ends)])  27 us
  transfers between devices with their start and end apart: 9, of which 5 were waited for; matrix products, arithmetic and copies ran while one was open for 12% of the time, Pallas kernels for 0%

commit v1 on v0

v1 whole, which is shorter than its diff:
```python
import functools
import math

import jax
import jax.numpy as jnp
from jax import lax
from jax.experimental import pallas as pl
from jax.experimental.pallas import tpu as pltpu
from jax.sharding import PartitionSpec as P

HALF_BAND = 512
ITERS = 3
EPS = 1e-05
SHRINK = 1.5
RING = 4
LANES = 128
WIDE = 256
EDGE = 4
PAD = 24
F32 = jnp.float32
BF16 = jnp.bfloat16
MESH = pl.DeviceIdType.MESH


def iota(shape, dim):
    return lax.broadcasted_iota(jnp.int32, shape, dim)


def kernel(
    geom,
    g_hbm, phen, ws_in,
    eff_out, ld_out,
    g_v, halo_l, halo_r, xh, xl, gram, p1, p2,
    st_x, st_l, st_r, st_e, ex_x, ex_e, red_a, red_b,
    mc, m2c, ppc, phic, mean, rinv, ws, vec, ld_acc,
    load_sem, halo_send, halo_recv, exs_x, exr_x, exs_e, exr_e,
    sa_send, sa_recv, sb_send, sb_recv, rs_send, p1_recv, p2_recv,
):
    nvar, near_count, far_count, samples = geom
    variants = nvar * ws_in.shape[0] * LANES
    tiles = ws_in.shape[0]
    width = tiles * LANES
    blocks = width // WIDE
    local = g_hbm.shape[0]
    chunks = local // LANES
    s = lax.axis_index("samp")
    d = lax.axis_index("var")
    near = lax.rem(d, near_count)
    far = lax.div(d, near_count)

    def samp_at(step):
        return lax.rem(s + step, RING)

    def var_at(step):
        return lax.rem(d + step + nvar, nvar)

    def dev(samp, var):
        return {"samp": samp, "var": var}

    ring_peers = [dev(samp_at(i), d) for i in range(1, RING)]
    right_edge = [dev(samp_at(i), var_at(1)) for i in range(RING)]
    left_edge = [dev(samp_at(i), var_at(-1)) for i in range(RING)]
    near_peers = [dev(s, far * near_count + lax.rem(near + i, near_count)) for i in range(1, near_count)]
    far_peers = [dev(s, lax.rem(far + i, far_count) * near_count + near) for i in range(1, far_count)]
    greeted = ring_peers + right_edge + left_edge + near_peers + far_peers

    def remote(src, dst, send, recv, device):
        copy = pltpu.make_async_remote_copy(
            src_ref=src, dst_ref=dst, send_sem=send, recv_sem=recv, device_id=device, device_id_type=MESH
        )
        copy.start()

    def drain(ref, sem):
        pltpu.make_async_copy(ref, ref, sem).wait()

    def load(c):
        rows = pl.ds(pl.multiple_of(c * LANES, LANES), LANES)
        return pltpu.make_async_copy(g_hbm.at[rows], g_v.at[rows], load_sem.at[c])

    for c in range(chunks):
        load(c).start()
    barrier = pltpu.get_barrier_semaphore()
    for peer in greeted:
        pl.semaphore_signal(barrier, inc=1, device_id=peer, device_id_type=MESH)
    pl.semaphore_wait(barrier, len(greeted))

    remote(g_hbm.at[:, pl.ds(width - WIDE, WIDE)], halo_l, halo_send.at[0], halo_recv.at[0], dev(s, var_at(1)))
    remote(g_hbm.at[:, pl.ds(0, WIDE)], halo_r, halo_send.at[1], halo_recv.at[1], dev(s, var_at(-1)))

    square = (LANES, LANES)
    eye = iota(square, 0) == iota(square, 1)
    lower = iota(square, 0) <= iota(square, 1)

    def to_column(row):
        return jnp.sum(jnp.where(eye, row, 0.0), axis=1, keepdims=True)

    def to_row(column):
        return jnp.sum(jnp.where(eye, column, 0.0), axis=0, keepdims=True)

    def chunk_stats(c, carry):
        load(c).wait()
        rows = pl.ds(pl.multiple_of(c * LANES, LANES), LANES)
        trait = phen[pl.ds(c, 1), :]
        phic[pl.ds(c, 1), :] = jnp.broadcast_to(jnp.sum(trait, axis=1, keepdims=True), (1, LANES))
        column = jnp.broadcast_to(to_column(trait), square)
        for t in range(tiles):
            values = g_v[rows, t * LANES : (t + 1) * LANES]
            centre = jnp.sum(values, axis=0, keepdims=True) * (1.0 / LANES)
            off = values - centre
            mc[c, t : t + 1, :] = centre
            m2c[c, t : t + 1, :] = jnp.sum(off * off, axis=0, keepdims=True)
            ppc[c, t : t + 1, :] = jnp.sum(off * column, axis=0, keepdims=True)
        return carry

    lax.fori_loop(0, chunks, chunk_stats, 0)

    own_mean = mc[0]
    for c in range(1, chunks):
        own_mean = own_mean + mc[c]
    own_mean = own_mean * (1.0 / chunks)
    own_m2 = jnp.zeros((tiles, LANES), F32)
    own_pp = jnp.zeros((tiles, LANES), F32)
    own_phi = jnp.zeros((1, LANES), F32)
    for c in range(chunks):
        shift = mc[c] - own_mean
        phi = phic[c : c + 1, :]
        own_m2 = own_m2 + m2c[c] + LANES * (shift * shift)
        own_pp = own_pp + ppc[c] + shift * phi
        own_phi = own_phi + phi

    mine = st_x.at[s]
    mine[...] = jnp.zeros((3 * PAD, LANES), F32)
    mine[2 : 2 + tiles, :] = own_mean
    mine[PAD + 2 : PAD + 2 + tiles, :] = own_m2
    mine[2 * PAD + 2 : 2 * PAD + 2 + tiles, :] = own_pp
    mine[2 * PAD + tiles + 4 : 2 * PAD + tiles + 5, :] = own_phi
    ws[...] = jnp.zeros((PAD, LANES), F32)
    ws[2 : 2 + tiles, :] = ws_in[...].astype(F32)
    for k in range(3):
        st_l[8 * k : 8 * k + 8, :] = mine[PAD * k : PAD * k + 8, :]
        st_r[8 * k : 8 * k + 8, :] = mine[PAD * k + 16 : PAD * k + 24, :]
    st_l[24:32, :] = ws[0:8, :]
    st_r[24:32, :] = ws[16:24, :]

    for peer in ring_peers:
        remote(st_x.at[s], st_x.at[s], exs_x.at[0], exr_x.at[0], peer)
    for i in range(RING):
        remote(st_r, st_e.at[s], exs_e.at[0], exr_e.at[0], right_edge[i])
    for i in range(RING):
        remote(st_l, st_e.at[RING + s], exs_e.at[0], exr_e.at[0], left_edge[i])

    grid_row = iota((PAD, LANES), 0)
    place = d * width - WIDE + grid_row * LANES + iota((PAD, LANES), 1)
    edge_rows = iota((8, LANES), 0) < EDGE

    def extend(centre, left, right):
        top = centre[0:8] + jnp.where(edge_rows, left, 0.0)
        bottom = centre[16:24] + jnp.where(edge_rows, right, 0.0)
        return jnp.concatenate([top, centre[8:16], bottom], axis=0)

    inside = grid_row < tiles + EDGE
    own = (grid_row >= 2) & (grid_row < tiles + 2)

    def combine(with_edges):
        parts = []
        for k in range(3):
            each = []
            for i in range(RING):
                centre = st_x[i, PAD * k : PAD * (k + 1), :]
                if with_edges:
                    centre = extend(centre, st_e[i, 8 * k : 8 * k + 8, :], st_e[RING + i, 8 * k : 8 * k + 8, :])
                each.append(centre)
            parts.append(each)
        means, squares, products = parts
        mu = (means[0] + means[1] + means[2] + means[3]) * (1.0 / RING)
        total = squares[0] + squares[1] + squares[2] + squares[3]
        joint = products[0] + products[1] + products[2] + products[3]
        for i in range(RING):
            shift = means[i] - mu
            phi = st_x[i, 2 * PAD + tiles + 4 : 2 * PAD + tiles + 5, :]
            total = total + local * (shift * shift)
            joint = joint + shift * phi
        spread = total * (1.0 / samples)
        scale = lax.rsqrt(spread + EPS)
        mean[...] = mu
        rinv[...] = scale * (1.0 / math.sqrt(samples))
        marginal = jnp.where(inside, joint * scale * (1.0 / math.sqrt(samples)), 0.0)
        return marginal, jnp.where(inside, spread * (scale * scale), 0.0)

    drain(st_x.at[pl.ds(0, 3)], exr_x.at[0])
    combine(False)

    def convert(source, lane, group):
        mu = [mean[pl.ds(2 * group + h, 1), :] for h in range(2)]
        scale = [rinv[pl.ds(2 * group + h, 1), :] for h in range(2)]

        def piece(c, carry):
            rows = pl.ds(pl.multiple_of(c * LANES, LANES), LANES)
            for h in range(2):
                begin = pl.multiple_of(lane + h * LANES, LANES)
                values = (source[rows, pl.ds(begin, LANES)] - mu[h]) * scale[h]
                top = values.astype(BF16)
                rest = (values - top.astype(F32)).astype(BF16)
                goal = pl.ds(pl.multiple_of(group * WIDE + h * LANES, LANES), LANES)
                xh[rows, goal] = top
                xl[rows, goal] = rest
            return carry

        lax.fori_loop(0, chunks, piece, 0)

    def convert_own(group):
        convert(g_v, pl.multiple_of((group - 1) * WIDE, WIDE), group)

    wide_row = iota((WIDE, WIDE), 0)
    wide_lane = iota((WIDE, WIDE), 1)
    wrap = wide_row > wide_lane
    first = d * width - WIDE

    def gram_block(i):
        pick = pl.ds(pl.multiple_of((i + 2) * WIDE, WIDE), WIDE)
        row_h = xh[:, pick].T
        row_l = xl[:, pick].T
        begin = jnp.concatenate(
            [to_column(ws[pl.ds(2 * i + 4, 1), :]), to_column(ws[pl.ds(2 * i + 5, 1), :])], axis=0
        )

        def product(t):
            near_pick = pl.ds(pl.multiple_of((i + t) * WIDE, WIDE), WIDE)
            col_h = xh[:, near_pick]
            col_l = xl[:, near_pick]
            dims = (((1,), (0,)), ((), ()))
            return (
                lax.dot_general(row_h, col_h, dims, preferred_element_type=F32)
                + lax.dot_general(row_h, col_l, dims, preferred_element_type=F32)
                + lax.dot_general(row_l, col_h, dims, preferred_element_type=F32)
            )

        at = (first + i * WIDE + wide_lane).astype(F32)
        values = jnp.where(wrap, product(2), product(0))
        gram[i, :, 0:WIDE] = jnp.where(jnp.where(wrap, at + HALF_BAND, at) >= begin, values, 0.0)
        gram[i, :, WIDE:HALF_BAND] = jnp.where(at + WIDE >= begin, product(1), 0.0)

    half = 32
    ahead = samp_at(1)
    behind = samp_at(3)
    across = samp_at(2)

    def band_rows(block, quarter, piece):
        return gram.at[block, pl.ds(pl.multiple_of(quarter * 64 + piece * half, half), half), :]

    def ring_send(i):
        remote(band_rows(i, across, 0), p1.at[0, i], rs_send, p1_recv.at[0, i], dev(ahead, d))
        remote(band_rows(i, across, 1), p1.at[1, i], rs_send, p1_recv.at[1, i], dev(behind, d))
        remote(band_rows(i, ahead, 1), p2.at[0, i, pl.ds(half, half), :], rs_send, p2_recv.at[0, i], dev(ahead, d))
        remote(band_rows(i, behind, 0), p2.at[1, i, pl.ds(0, half), :], rs_send, p2_recv.at[1, i], dev(behind, d))

    def ring_relay(i):
        drain(p1.at[0, i], p1_recv.at[0, i])
        p1[0, i] = p1[0, i] + gram[i, pl.ds(pl.multiple_of(ahead * 64, half), half), :]
        remote(p1.at[0, i], p2.at[0, i, pl.ds(0, half), :], rs_send, p2_recv.at[0, i], dev(ahead, d))
        drain(p1.at[1, i], p1_recv.at[1, i])
        p1[1, i] = p1[1, i] + gram[i, pl.ds(pl.multiple_of(behind * 64 + half, half), half), :]
        remote(p1.at[1, i], p2.at[1, i, pl.ds(half, half), :], rs_send, p2_recv.at[1, i], dev(behind, d))

    for group in (1, 2, 3):
        convert_own(group)

    def inner(i, carry):
        gram_block(i)
        ring_send(i)

        @pl.when(i + 3 <= blocks)
        def _():
            convert_own(i + 3)

        @pl.when(i > 1)
        def _():
            ring_relay(i - 1)

        return carry

    lax.fori_loop(1, blocks - 1, inner, 0)

    drain(st_e, exr_e.at[0])
    marginal, diag = combine(True)
    ws_ext = ws[...]
    ws_bottom = ws_ext[16:24] + jnp.where(edge_rows, st_e[RING, 24:32, :], 0.0)
    ws[16:24, :] = ws_bottom + jnp.where(place[16:24] >= variants, F32(variants), 0.0)
    drain(halo_l, halo_recv.at[0])
    convert(halo_l, 0, 0)
    gram_block(0)
    ring_send(0)
    ring_relay(blocks - 2)
    drain(halo_r, halo_recv.at[1])
    convert(halo_r, 0, blocks + 1)
    gram_block(blocks - 1)
    ring_send(blocks - 1)
    ring_relay(0)

    def apply_part(e):
        out = ex_x.at[e, s]
        out[...] = jnp.zeros((PAD, LANES), F32)

        def block(i, carry):
            for a in range(2):
                column = to_column(vec[pl.ds(2 * i + 4 + a, 1), :])
                lines = jnp.zeros(square, F32)
                for b in range(4):
                    cells = gram[i, a * LANES : (a + 1) * LANES, b * LANES : (b + 1) * LANES]
                    low = pl.ds(2 * i + b, 1)
                    high = pl.ds(2 * i + b + 4, 1)
                    across_cells = cells * column
                    if b >= 2 or a < b:
                        lines = lines + cells * vec[low, :]
                        out[low, :] = out[low, :] + jnp.sum(across_cells, axis=0, keepdims=True)
                    elif a > b:
                        lines = lines + cells * vec[high, :]
                        out[high, :] = out[high, :] + jnp.sum(across_cells, axis=0, keepdims=True)
                    else:
                        lines = lines + cells * jnp.where(lower, vec[low, :], vec[high, :])
                        out[low, :] = out[low, :] + jnp.sum(jnp.where(lower, across_cells, 0.0), axis=0, keepdims=True)
                        out[high, :] = out[high, :] + jnp.sum(jnp.where(lower, 0.0, across_cells), axis=0, keepdims=True)
                here = pl.ds(2 * i + 4 + a, 1)
                out[here, :] = out[here, :] + to_row(jnp.sum(lines, axis=1, keepdims=True))
            return carry

        lax.fori_loop(0, blocks, block, 0)

    def trade(e):
        src = ex_x.at[e, s]
        for peer in ring_peers:
            remote(src, src, exs_x.at[e + 1], exr_x.at[e + 1], peer)
        for i in range(RING):
            remote(src.at[pl.ds(16, 8)], ex_e.at[e, s], exs_e.at[e + 1], exr_e.at[e + 1], right_edge[i])
        for i in range(RING):
            remote(src.at[pl.ds(0, 8)], ex_e.at[e, RING + s], exs_e.at[e + 1], exr_e.at[e + 1], left_edge[i])

    def gather(e):
        drain(ex_x.at[e, pl.ds(0, 3)], exr_x.at[e + 1])
        drain(ex_e.at[e], exr_e.at[e + 1])
        total = extend(ex_x[e, 0], ex_e[e, 0], ex_e[e, RING])
        for i in range(1, RING):
            total = total + extend(ex_x[e, i], ex_e[e, i], ex_e[e, RING + i])
        return total

    def dots_send(r, pairs):
        rows = [jnp.sum(jnp.where(own, a * b, 0.0), axis=0, keepdims=True) for a, b in pairs]
        rows.append(jnp.zeros((8 - len(rows), LANES), F32))
        red_a[r, near] = jnp.concatenate(rows, axis=0)
        for peer in near_peers:
            remote(red_a.at[r, near], red_a.at[r, near], sa_send.at[r], sa_recv.at[r], peer)

    def dots_pass(r):
        drain(red_a.at[r, pl.ds(0, near_count - 1)], sa_recv.at[r])
        total = red_a[r, 0]
        for i in range(1, near_count):
            total = total + red_a[r, i]
        red_b[r, far] = total
        for peer in far_peers:
            remote(red_b.at[r, far], red_b.at[r, far], sb_send.at[r], sb_recv.at[r], peer)

    def dots_end(r):
        drain(red_b.at[r, pl.ds(0, far_count - 1)], sb_recv.at[r])
        total = red_b[r, 0]
        for i in range(1, far_count):
            total = total + red_b[r, i]
        sums = jnp.broadcast_to(jnp.sum(total, axis=1, keepdims=True), (8, LANES))
        return [sums[k : k + 1] for k in range(3)]

    weight = diag + SHRINK
    vec[...] = marginal
    apply_part(0)
    trade(0)
    ring_relay(blocks - 1)
    image0 = gather(0) + weight * marginal
    dots_send(0, [(marginal, marginal), (marginal, image0)])
    vec[...] = image0
    apply_part(1)
    trade(1)
    dots_pass(0)
    image1 = gather(1) + weight * image0
    rr0, curve0 = dots_end(0)[:2]
    alpha0 = rr0 / curve0
    res1 = marginal - alpha0 * image0
    ares1 = image0 - alpha0 * image1
    dots_send(1, [(res1, res1), (res1, ares1), (res1, image0)])
    vec[...] = image1
    apply_part(2)
    trade(2)
    dots_pass(1)
    image2 = gather(2) + weight * image1
    rr1, inner1, cross1 = dots_end(1)
    beta0 = rr1 / rr0
    curve1 = inner1 + beta0 * (cross1 + cross1) + beta0 * beta0 * curve0
    alpha1 = rr1 / curve1
    dir1 = res1 + beta0 * marginal
    adir1 = ares1 + beta0 * image0
    res2 = res1 - alpha1 * adir1
    aares1 = image1 - alpha0 * image2
    ares2 = ares1 - alpha1 * (aares1 + beta0 * image1)
    dots_send(2, [(res2, res2), (res2, ares2), (res2, adir1)])
    dots_pass(2)
    rr2, inner2, cross2 = dots_end(2)
    beta1 = rr2 / rr1
    curve2 = inner2 + beta1 * (cross2 + cross2) + beta1 * beta1 * curve1
    alpha2 = rr2 / curve2
    dir2 = res2 + beta1 * dir1
    effects = alpha0 * marginal + alpha1 * dir1 + alpha2 * dir2
    eff_out[...] = effects[2 : 2 + tiles]

    ld_acc[...] = jnp.zeros((PAD, LANES), F32)
    local_row = iota((64, LANES), 0)
    local_lane = iota((64, LANES), 1)
    spot = lax.rem(s, 2) * 64
    tile_of = lax.div(s, 2)

    def finish(i, carry):
        drain(p2.at[0, i], p2_recv.at[0, i])
        drain(p2.at[1, i], p2_recv.at[1, i])
        rows = pl.ds(pl.multiple_of(s * 64, 64), 64)
        lines = jnp.zeros((64, LANES), F32)
        for b in range(4):
            cols = slice(b * LANES, (b + 1) * LANES)
            cells = gram[i, rows, cols] + p2[0, i, :, cols] + p2[1, i, :, cols]
            cells = cells * cells
            lines = lines + cells
            low = pl.ds(2 * i + b, 1)
            if b >= 2:
                ld_acc[low, :] = ld_acc[low, :] + jnp.sum(cells, axis=0, keepdims=True)
            else:
                high = pl.ds(2 * i + b + 4, 1)
                before = s * 64 + local_row <= b * LANES + local_lane
                ld_acc[low, :] = ld_acc[low, :] + jnp.sum(jnp.where(before, cells, 0.0), axis=0, keepdims=True)
                ld_acc[high, :] = ld_acc[high, :] + jnp.sum(jnp.where(before, 0.0, cells), axis=0, keepdims=True)
        column = jnp.sum(lines, axis=1, keepdims=True)
        row = jnp.sum(jnp.where(local_row + spot == local_lane, column, 0.0), axis=0, keepdims=True)
        here = pl.ds(2 * i + 4 + tile_of, 1)
        ld_acc[here, :] = ld_acc[here, :] + row
        return carry

    lax.fori_loop(0, blocks, finish, 0)
    ex_x[3, s] = ld_acc[...]
    trade(3)
    scores = gather(3) + diag * diag
    ld_out[...] = scores[2 : 2 + tiles]

    drain(halo_l, halo_send.at[0])
    drain(halo_r, halo_send.at[1])
    drain(st_x.at[pl.ds(0, 3)], exs_x.at[0])
    drain(st_e, exs_e.at[0])
    for e in range(4):
        drain(ex_x.at[e, pl.ds(0, 3)], exs_x.at[e + 1])
        drain(ex_e.at[e], exs_e.at[e + 1])
    for r in range(3):
        drain(red_a.at[r, pl.ds(0, near_count - 1)], sa_send.at[r])
        drain(red_b.at[r, pl.ds(0, far_count - 1)], sb_send.at[r])
    drain(gram.at[pl.ds(0, 3 * blocks // 4)], rs_send)


def shards(nvar, genotypes, phenotype, win_start, win_end):
    local, width = genotypes.shape
    near = 8 if nvar % 8 == 0 and nvar > 8 else 2
    far = nvar // near
    tiles = width // LANES
    blocks = width // WIDE
    chunks = local // LANES
    geom = (nvar, near, far, local * RING)
    vmem = pl.BlockSpec(memory_space=pltpu.VMEM)
    dma = pltpu.SemaphoreType.DMA
    effects, scores = pl.pallas_call(
        functools.partial(kernel, geom),
        out_shape=[jax.ShapeDtypeStruct((tiles, LANES), F32)] * 2,
        in_specs=[pl.BlockSpec(memory_space=pl.ANY), vmem, vmem],
        out_specs=[vmem, vmem],
        scratch_shapes=[
            pltpu.VMEM((local, width), F32),
            pltpu.VMEM((local, WIDE), F32),
            pltpu.VMEM((local, WIDE), F32),
            pltpu.VMEM((local, width + 2 * WIDE), BF16),
            pltpu.VMEM((local, width + 2 * WIDE), BF16),
            pltpu.VMEM((blocks, WIDE, HALF_BAND), F32),
            pltpu.VMEM((2, blocks, 32, HALF_BAND), F32),
            pltpu.VMEM((2, blocks, 64, HALF_BAND), F32),
            pltpu.VMEM((RING, 3 * PAD, LANES), F32),
            pltpu.VMEM((32, LANES), F32),
            pltpu.VMEM((32, LANES), F32),
            pltpu.VMEM((2 * RING, 32, LANES), F32),
            pltpu.VMEM((4, RING, PAD, LANES), F32),
            pltpu.VMEM((4, 2 * RING, 8, LANES), F32),
            pltpu.VMEM((3, near, 8, LANES), F32),
            pltpu.VMEM((3, far, 8, LANES), F32),
            pltpu.VMEM((chunks, tiles, LANES), F32),
            pltpu.VMEM((chunks, tiles, LANES), F32),
            pltpu.VMEM((chunks, tiles, LANES), F32),
            pltpu.VMEM((chunks, LANES), F32),
            pltpu.VMEM((PAD, LANES), F32),
            pltpu.VMEM((PAD, LANES), F32),
            pltpu.VMEM((PAD, LANES), F32),
            pltpu.VMEM((PAD, LANES), F32),
            pltpu.VMEM((PAD, LANES), F32),
            dma((chunks,)),
            dma((2,)),
            dma((2,)),
            dma((5,)),
            dma((5,)),
            dma((5,)),
            dma((5,)),
            dma((3,)),
            dma((3,)),
            dma((3,)),
            dma((3,)),
            dma,
            dma((2, blocks)),
            dma((2, blocks)),
        ],
        compiler_params=pltpu.CompilerParams(
            collective_id=0, has_side_effects=True, vmem_limit_bytes=48 * 1024 * 1024
        ),
    )(genotypes, phenotype.reshape(chunks, LANES), win_start.reshape(tiles, LANES))
    return effects.reshape(width), scores.reshape(width)


def solution(mesh):
    in_specs = (P("samp", "var"), P("samp"), P("var"), P("var"))
    out_specs = (P("var"), P("var"))
    body = functools.partial(shards, mesh.shape["var"])
    return jax.shard_map(body, mesh=mesh, in_specs=in_specs, out_specs=out_specs, check_vma=False)
```

time: 980 us -> 83.7 us (0.09)
  blocking collectives: 352 us -> 0 us
  local copies, waits for them, and re-layouts: 320 us -> 2.58 us
  matrix products: 143 us -> 0 us
  Pallas kernels: 0 us -> 79.3 us
  waiting for transfers between devices: 67.8 us -> 0 us
  starting transfers between devices: 32.6 us -> 0 us
  other arithmetic: 31.5 us -> 0 us
  between operations: 21.1 us -> 0.65 us
  loops' own time: 10.6 us -> 0 us
    psum x8 -> x0, blocking collectives: 352 us -> none  [the longest x3 194 us: squares_of(): return lax.psum(jnp.sum(residual * residual), 'var')]
    gather x3 -> x0, local copies, waits for them, and re-layouts: 305 us -> none  [shards(): windows = wide[picks]]
    dot_general x20 -> x0, matrix products: 143 us -> none  [the longest x16 98 us: one_block(): lax.dot_general(rows, near, (((0,), (0,)), ((), ())), precision=HIGH, pre...]
    pallas_call x0 -> x1, Pallas kernels: none -> 79.3 us  [shards(): pl.pallas_call(functools.partial(kernel, geom), out_shape=[jax.ShapeDtype...]
    psum x1 -> x0, waiting for transfers between devices: 56.9 us -> none  [shards(): band_sum, marginal_sum = lax.psum((partial_value, local_marginal), 'samp')]
    ppermute x8 -> x0, starting transfers between devices: 32.6 us -> none  [the longest x4 27 us: padded(): lax.ppermute(tail, axis, [(i, (i + 1) % count) for i in range(ends)])]
    reduce_sum x8 -> x0, other arithmetic: 16.9 us -> none  [the longest x1 5.7 us: shards(): score_part = jnp.sum(band * band, axis=2).reshape(blocks * BLOCK)]
    ppermute x8 -> x0, waiting for transfers between devices: 10.9 us -> none  [the longest x4 8.36 us: padded(): lax.ppermute(head, axis, [((i + 1) % count, i) for i in range(ends)])]
  transfers between devices with their start and end apart: 9 -> 0, of which waited for: 5 -> 0; matrix products, arithmetic and copies ran while one was open for 12% -> 0% of each run, Pallas kernels for 0% -> 0%
where the time goes in v1:
time: 83.7 us; the launch traced here: 82.5 us
  Pallas kernels  79.3 us (95%)
  local copies, waits for them, and re-layouts  2.58 us (3%)
    pallas_call x1, Pallas kernels, shards(): pl.pallas_call(functools.partial(kernel, geom), out_shape=[jax.ShapeDtype...  79.3 us
    unnamed x6, local copies, waits for them, and re-layouts  2.58 us

profile of v1, /device:TPU:0, one launch (start us, length us, event | category | flops | bytes accessed | tf_op | source)
XLA Modules:
  0.0 82.5 jit_solution(5346939183589881473)
XLA Ops:
  0.6 0.0 copy-start
  0.6 0.7 copy-done
  1.3 0.0 copy-start.1
  1.3 0.7 copy-done.1
  2.0 79.3 %shard_map.50 = (f32[16,128]{1,0:T(8,128)S(1)}, f32[16,128]{1,0:T(8,128)S(1)}) custom-call(f32[1024,2048]{1,0:T(8,128)} %g_hbm.1, f32[8,128]{1,0:T(8,128)S(1)} %bitcast.7, s32[16,128]{1,0:T(8,128)S(1)} %bitcast.4), custom_call_target="tpu_custom_call" | custom-call | tf_op jit(solution)/shard_map/pallas_call | solution.py:470
  81.3 0.6 copy.7
  81.9 0.6 copy.8
Async XLA Ops:
  0.6 0.7 copy-start
  1.3 0.7 copy-start.1

commit v2 on v1

v2 whole, which is shorter than its diff:
```python
import functools
import math

import jax
import jax.numpy as jnp
from jax import lax
from jax.experimental import pallas as pl
from jax.experimental.pallas import tpu as pltpu
from jax.sharding import PartitionSpec as P

HALF_BAND = 512
ITERS = 3
EPS = 1e-05
SHRINK = 1.5
RING = 4
LANES = 128
WIDE = 256
EDGE = 4
PAD = 24
F32 = jnp.float32
BF16 = jnp.bfloat16
MESH = pl.DeviceIdType.MESH


def iota(shape, dim):
    return lax.broadcasted_iota(jnp.int32, shape, dim)


def kernel(
    geom,
    g_hbm, phen_hbm, ws_hbm,
    eff_out, ld_out,
    g_v, halo_l, halo_r, xh, xl, gram, band, p1, p2,
    phen, phcol, ws_in,
    st_x, st_l, st_r, st_e, ex_x, ex_e, red_a, red_b,
    delta, rinv, ws, spots, vec, ld_acc, sides,
    load_sem, small_sem, halo_send, halo_recv, exs_x, exr_x, exs_e, exr_e,
    sa_send, sa_recv, sb_send, sb_recv, rs_send, p1_recv, p2_recv,
):
    nvar, near_count, far_count, samples = geom
    tiles = ws_in.shape[0]
    width = tiles * LANES
    variants = nvar * width
    blocks = width // WIDE
    local = g_hbm.shape[0]
    chunks = local // LANES
    s = lax.axis_index("samp")
    d = lax.axis_index("var")
    near = lax.rem(d, near_count)
    far = lax.div(d, near_count)

    def samp_at(step):
        return lax.rem(s + step, RING)

    def var_at(step):
        return lax.rem(d + step + nvar, nvar)

    def dev(samp, var):
        return {"samp": samp, "var": var}

    ring_peers = [dev(samp_at(i), d) for i in range(1, RING)]
    right_edge = [dev(samp_at(i), var_at(1)) for i in range(RING)]
    left_edge = [dev(samp_at(i), var_at(-1)) for i in range(RING)]
    near_peers = [dev(s, far * near_count + lax.rem(near + i, near_count)) for i in range(1, near_count)]
    far_peers = [dev(s, lax.rem(far + i, far_count) * near_count + near) for i in range(1, far_count)]
    greeted = ring_peers + right_edge + left_edge + near_peers + far_peers

    def remote(src, dst, send, recv, device):
        copy = pltpu.make_async_remote_copy(
            src_ref=src, dst_ref=dst, send_sem=send, recv_sem=recv, device_id=device, device_id_type=MESH
        )
        copy.start()

    def drain(ref, sem):
        pltpu.make_async_copy(ref, ref, sem).wait()

    def load(group):
        cols = pl.ds(pl.multiple_of((group - 1) * WIDE, WIDE), WIDE)
        return pltpu.make_async_copy(g_hbm.at[:, cols], g_v.at[:, cols], load_sem.at[group - 1])

    small = [
        pltpu.make_async_copy(phen_hbm, phen, small_sem.at[0]),
        pltpu.make_async_copy(ws_hbm, ws_in, small_sem.at[1]),
    ]
    for copy in small:
        copy.start()
    for group in range(1, blocks + 1):
        load(group).start()
    barrier = pltpu.get_barrier_semaphore()
    for peer in greeted:
        pl.semaphore_signal(barrier, inc=1, device_id=peer, device_id_type=MESH)

    square = (LANES, LANES)
    eye = iota(square, 0) == iota(square, 1)
    lower = iota(square, 0) <= iota(square, 1)

    def to_column(row):
        return jnp.sum(jnp.where(eye, row, 0.0), axis=1, keepdims=True)

    def to_row(column):
        return jnp.sum(jnp.where(eye, column, 0.0), axis=0, keepdims=True)

    for copy in small:
        copy.wait()
    own_phi = jnp.zeros((1, 1), F32)
    for c in range(chunks):
        trait = phen[c : c + 1, :]
        own_phi = own_phi + jnp.sum(trait, axis=1, keepdims=True)
        phcol[c * LANES : (c + 1) * LANES, :] = jnp.broadcast_to(to_column(trait), square)
    mine = st_x.at[s]
    mine[...] = jnp.zeros((3 * PAD, LANES), F32)
    ws[...] = jnp.zeros((PAD, LANES), F32)
    ws[2 : 2 + tiles, :] = ws_in[...].astype(F32)

    def prepare(source, lane, group, keep):
        def rows_of(c):
            return pl.ds(pl.multiple_of(c * LANES, LANES), LANES)

        for h in range(2):
            cols = pl.ds(pl.multiple_of(lane + h * LANES, LANES), LANES)
            goal = pl.ds(pl.multiple_of(group * WIDE + h * LANES, LANES), LANES)

            def add(c, total):
                return total + jnp.sum(source[rows_of(c), cols].reshape(LANES // 8, 8, LANES), axis=0)

            total = lax.fori_loop(0, chunks, add, jnp.zeros((8, LANES), F32), unroll=True)
            centre = jnp.sum(total, axis=0, keepdims=True) * (1.0 / local)

            def split(c, carry):
                sq, pp = carry
                rows = rows_of(c)
                off = source[rows, cols] - centre
                top = off.astype(BF16)
                xh[rows, goal] = top
                xl[rows, goal] = (off - top.astype(F32)).astype(BF16)
                if keep:
                    sq = sq + jnp.sum((off * off).reshape(LANES // 8, 8, LANES), axis=0)
                    pp = pp + jnp.sum((off * phcol[rows, :]).reshape(LANES // 8, 8, LANES), axis=0)
                return sq, pp

            start = (jnp.zeros((8, LANES), F32), jnp.zeros((8, LANES), F32))
            sq, pp = lax.fori_loop(0, chunks, split, start)
            if keep:
                line = 2 * group + h
                mine[pl.ds(line, 1), :] = centre
                mine[pl.ds(PAD + line, 1), :] = jnp.sum(sq, axis=0, keepdims=True)
                mine[pl.ds(2 * PAD + line, 1), :] = jnp.sum(pp, axis=0, keepdims=True)

    def prepare_own(group, carry):
        load(group).wait()
        prepare(g_v, pl.multiple_of((group - 1) * WIDE, WIDE), group, True)
        return carry

    lax.fori_loop(1, blocks + 1, prepare_own, 0)
    mine[2 * PAD + tiles + 4 : 2 * PAD + tiles + 5, :] = jnp.broadcast_to(own_phi, (1, LANES))
    for k in range(3):
        st_l[8 * k : 8 * k + 8, :] = mine[PAD * k : PAD * k + 8, :]
        st_r[8 * k : 8 * k + 8, :] = mine[PAD * k + 16 : PAD * k + 24, :]
    st_l[24:32, :] = ws[0:8, :]
    st_r[24:32, :] = ws[16:24, :]

    pl.semaphore_wait(barrier, len(greeted))
    remote(g_hbm.at[:, pl.ds(width - WIDE, WIDE)], halo_l, halo_send.at[0], halo_recv.at[0], dev(s, var_at(1)))
    remote(g_hbm.at[:, pl.ds(0, WIDE)], halo_r, halo_send.at[1], halo_recv.at[1], dev(s, var_at(-1)))
    for peer in ring_peers:
        remote(st_x.at[s], st_x.at[s], exs_x.at[0], exr_x.at[0], peer)
    for i in range(RING):
        remote(st_r, st_e.at[s], exs_e.at[0], exr_e.at[0], right_edge[i])
    for i in range(RING):
        remote(st_l, st_e.at[RING + s], exs_e.at[0], exr_e.at[0], left_edge[i])

    wrap = iota((WIDE, WIDE), 0) > iota((WIDE, WIDE), 1)

    def gram_block(i):
        pick = pl.ds(pl.multiple_of((i + 2) * WIDE, WIDE), WIDE)
        row_h = xh[:, pick].T
        row_l = xl[:, pick].T

        def product(t):
            near_pick = pl.ds(pl.multiple_of((i + t) * WIDE, WIDE), WIDE)
            col_h = xh[:, near_pick]
            col_l = xl[:, near_pick]
            dims = (((1,), (0,)), ((), ()))
            return (
                lax.dot_general(row_h, col_h, dims, preferred_element_type=F32)
                + lax.dot_general(row_h, col_l, dims, preferred_element_type=F32)
                + lax.dot_general(row_l, col_h, dims, preferred_element_type=F32)
            )

        gram[i, :, 0:WIDE] = jnp.where(wrap, product(2), product(0))
        gram[i, :, WIDE:HALF_BAND] = product(1)

    half = 32
    ahead = samp_at(1)
    behind = samp_at(3)
    across = samp_at(2)

    def band_rows(block, quarter, piece):
        return gram.at[block, pl.ds(pl.multiple_of(quarter * 64 + piece * half, half), half), :]

    def send_far(i):
        remote(band_rows(i, across, 0), p1.at[0, i], rs_send, p1_recv.at[0, i], dev(ahead, d))
        remote(band_rows(i, across, 1), p1.at[1, i], rs_send, p1_recv.at[1, i], dev(behind, d))

    def send_direct(i):
        remote(band_rows(i, ahead, 1), p2.at[0, i, pl.ds(half, half), :], rs_send, p2_recv.at[0, i], dev(ahead, d))
        remote(band_rows(i, behind, 0), p2.at[1, i, pl.ds(0, half), :], rs_send, p2_recv.at[1, i], dev(behind, d))

    def relay(i):
        drain(p1.at[0, i], p1_recv.at[0, i])
        p1[0, i] = p1[0, i] + gram[i, pl.ds(pl.multiple_of(ahead * 64, half), half), :]
        remote(p1.at[0, i], p2.at[0, i, pl.ds(0, half), :], rs_send, p2_recv.at[0, i], dev(ahead, d))
        drain(p1.at[1, i], p1_recv.at[1, i])
        p1[1, i] = p1[1, i] + gram[i, pl.ds(pl.multiple_of(behind * 64 + half, half), half), :]
        remote(p1.at[1, i], p2.at[1, i, pl.ds(half, half), :], rs_send, p2_recv.at[1, i], dev(behind, d))

    def inner(i, carry):
        gram_block(i)
        send_far(i)

        @pl.when(i >= 5)
        def _():
            relay(i - 4)

        return carry

    lax.fori_loop(1, blocks - 1, inner, 0)

    grid_row = iota((PAD, LANES), 0)
    place = d * width - WIDE + grid_row * LANES + iota((PAD, LANES), 1)
    edge_rows = iota((8, LANES), 0) < EDGE
    inside = grid_row < tiles + EDGE
    own = (grid_row >= 2) & (grid_row < tiles + 2)

    def extend(centre, left, right):
        top = centre[0:8] + jnp.where(edge_rows, left, 0.0)
        bottom = centre[16:24] + jnp.where(edge_rows, right, 0.0)
        return jnp.concatenate([top, centre[8:16], bottom], axis=0)

    drain(st_x.at[pl.ds(0, 3)], exr_x.at[0])
    drain(st_e, exr_e.at[0])

    def stat(k, i):
        return extend(
            st_x[i, PAD * k : PAD * (k + 1), :],
            st_e[i, 8 * k : 8 * k + 8, :],
            st_e[RING + i, 8 * k : 8 * k + 8, :],
        )

    means = [stat(0, i) for i in range(RING)]
    mu = (means[0] + means[1] + means[2] + means[3]) * (1.0 / RING)
    total = stat(1, 0) + stat(1, 1) + stat(1, 2) + stat(1, 3)
    joint = stat(2, 0) + stat(2, 1) + stat(2, 2) + stat(2, 3)
    for i in range(RING):
        shift = means[i] - mu
        delta[i] = shift
        phi = st_x[i, 2 * PAD + tiles + 4 : 2 * PAD + tiles + 5, :]
        total = total + local * (shift * shift)
        joint = joint + shift * phi
    spread = total * (1.0 / samples)
    scale = lax.rsqrt(spread + EPS)
    rinv[...] = scale
    spots[...] = place.astype(F32)
    marginal = jnp.where(inside, joint * scale * (1.0 / math.sqrt(samples)), 0.0)
    diag = jnp.where(inside, spread * (scale * scale), 0.0)
    ws_bottom = ws[16:24, :] + jnp.where(edge_rows, st_e[RING, 24:32, :], 0.0)
    ws[16:24, :] = ws_bottom + jnp.where(place[16:24] >= variants, F32(variants), 0.0)

    def mask_block(i):
        for a in range(2):
            here = pl.ds(2 * i + 4 + a, 1)
            begin = to_column(ws[here, :])
            shift = to_column(delta[s, here, :]) * float(local)
            for b in range(4):
                tile = (slice(a * LANES, (a + 1) * LANES), slice(b * LANES, (b + 1) * LANES))
                low = pl.ds(2 * i + b, 1)
                high = pl.ds(2 * i + b + 4, 1)
                if b >= 2 or a < b:
                    other, at = delta[s, low, :], spots[low, :]
                elif a > b:
                    other, at = delta[s, high, :], spots[high, :]
                else:
                    other = jnp.where(lower, delta[s, low, :], delta[s, high, :])
                    at = jnp.where(lower, spots[low, :], spots[high, :])
                cells = gram[i, tile[0], tile[1]] + shift * other
                band[i, tile[0], tile[1]] = jnp.where(at >= begin, cells, 0.0)

    def mask_inner(i, carry):
        mask_block(i)
        return carry

    lax.fori_loop(1, blocks - 1, mask_inner, 0)

    def apply_block(e, i):
        out = ex_x.at[e, s]
        for a in range(2):
            here = pl.ds(2 * i + 4 + a, 1)
            column = to_column(vec[here, :])
            lines = jnp.zeros(square, F32)
            for b in range(4):
                cells = band[i, a * LANES : (a + 1) * LANES, b * LANES : (b + 1) * LANES]
                low = pl.ds(2 * i + b, 1)
                high = pl.ds(2 * i + b + 4, 1)
                moved = cells * column
                if b >= 2 or a < b:
                    lines = lines + cells * vec[low, :]
                    out[low, :] = out[low, :] + jnp.sum(moved, axis=0, keepdims=True)
                elif a > b:
                    lines = lines + cells * vec[high, :]
                    out[high, :] = out[high, :] + jnp.sum(moved, axis=0, keepdims=True)
                else:
                    lines = lines + cells * jnp.where(lower, vec[low, :], vec[high, :])
                    out[low, :] = out[low, :] + jnp.sum(jnp.where(lower, moved, 0.0), axis=0, keepdims=True)
                    out[high, :] = out[high, :] + jnp.sum(jnp.where(lower, 0.0, moved), axis=0, keepdims=True)
            out[here, :] = out[here, :] + to_row(jnp.sum(lines, axis=1, keepdims=True))

    def apply_centre(e):
        ex_x[e, s] = jnp.zeros((PAD, LANES), F32)

        def block(i, carry):
            apply_block(e, i)
            return carry

        lax.fori_loop(2, blocks - 2, block, 0)

    def apply_sides(e):
        def block(n, carry):
            apply_block(e, n + (blocks - 4) * lax.div(n, 2))
            return carry

        lax.fori_loop(0, 4, block, 0)

    def trade_edges(e, first=None, last=None):
        first = ex_x.at[e, s, pl.ds(0, 8)] if first is None else first
        last = ex_x.at[e, s, pl.ds(16, 8)] if last is None else last
        for i in range(RING):
            remote(last, ex_e.at[e, s], exs_e.at[e + 1], exr_e.at[e + 1], right_edge[i])
        for i in range(RING):
            remote(first, ex_e.at[e, RING + s], exs_e.at[e + 1], exr_e.at[e + 1], left_edge[i])

    def trade_ring(e):
        for peer in ring_peers:
            remote(ex_x.at[e, s], ex_x.at[e, s], exs_x.at[e + 1], exr_x.at[e + 1], peer)

    def gather_ring(e):
        drain(ex_x.at[e, pl.ds(0, 3)], exr_x.at[e + 1])
        return (ex_x[e, 0] + ex_x[e, 1]) + (ex_x[e, 2] + ex_x[e, 3])

    def gather_edges(e, total):
        drain(ex_e.at[e], exr_e.at[e + 1])
        left = (ex_e[e, 0] + ex_e[e, 1]) + (ex_e[e, 2] + ex_e[e, 3])
        right = (ex_e[e, 4] + ex_e[e, 5]) + (ex_e[e, 6] + ex_e[e, 7])
        return extend(total, left, right)

    def dots_send(r, pairs):
        rows = [jnp.sum(jnp.where(own, a * b, 0.0), axis=0, keepdims=True) for a, b in pairs]
        rows.append(jnp.zeros((8 - len(rows), LANES), F32))
        red_a[r, near] = jnp.concatenate(rows, axis=0)
        for peer in near_peers:
            remote(red_a.at[r, near], red_a.at[r, near], sa_send.at[r], sa_recv.at[r], peer)

    def dots_pass(r):
        drain(red_a.at[r, pl.ds(0, near_count - 1)], sa_recv.at[r])
        total = red_a[r, 0]
        for i in range(1, near_count):
            total = total + red_a[r, i]
        red_b[r, far] = total
        for peer in far_peers:
            remote(red_b.at[r, far], red_b.at[r, far], sb_send.at[r], sb_recv.at[r], peer)

    def dots_end(r):
        drain(red_b.at[r, pl.ds(0, far_count - 1)], sb_recv.at[r])
        total = red_b[r, 0]
        for i in range(1, far_count):
            total = total + red_b[r, i]
        sums = jnp.broadcast_to(jnp.sum(total, axis=1, keepdims=True), (8, LANES))
        return [sums[k : k + 1] for k in range(3)]

    weight = diag + SHRINK
    outer = scale * (1.0 / samples)

    vec[...] = scale * marginal
    apply_centre(0)
    drain(halo_l, halo_recv.at[0])
    prepare(halo_l, 0, 0, False)
    gram_block(0)
    drain(halo_r, halo_recv.at[1])
    prepare(halo_r, 0, blocks + 1, False)
    gram_block(blocks - 1)
    mask_block(0)
    mask_block(blocks - 1)
    apply_sides(0)
    trade_edges(0)
    trade_ring(0)
    send_far(0)
    send_far(blocks - 1)
    for i in range(3, blocks - 2):
        relay(i)

    part = gather_ring(0)
    vec[...] = scale * (outer * part + weight * marginal)
    apply_centre(1)
    image0 = outer * gather_edges(0, part) + weight * marginal
    vec[...] = scale * image0
    apply_sides(1)
    trade_edges(1)
    trade_ring(1)
    dots_send(0, [(marginal, marginal), (marginal, image0)])
    relay(blocks - 2)
    relay(0)
    relay(blocks - 1)
    send_direct(1)
    dots_pass(0)

    part = gather_ring(1)
    vec[...] = scale * (outer * part + weight * image0)
    apply_centre(2)
    image1 = outer * gather_edges(1, part) + weight * image0
    vec[...] = scale * image1
    apply_sides(2)
    trade_edges(2)
    trade_ring(2)
    for i in (blocks - 2, 0, blocks - 1):
        send_direct(i)
    for i in range(2, blocks - 2):
        send_direct(i)
    rr0, curve0 = dots_end(0)[:2]
    alpha0 = rr0 / curve0
    res1 = marginal - alpha0 * image0
    ares1 = image0 - alpha0 * image1
    dots_send(1, [(res1, res1), (res1, ares1), (res1, image0)])
    dots_pass(1)

    part = gather_ring(2)
    image2 = outer * gather_edges(2, part) + weight * image1
    rr1, inner1, cross1 = dots_end(1)
    beta0 = rr1 / rr0
    curve1 = inner1 + beta0 * (cross1 + cross1) + beta0 * beta0 * curve0
    alpha1 = rr1 / curve1
    dir1 = res1 + beta0 * marginal
    adir1 = ares1 + beta0 * image0
    res2 = res1 - alpha1 * adir1
    aares1 = image1 - alpha0 * image2
    ares2 = ares1 - alpha1 * (aares1 + beta0 * image1)
    dots_send(2, [(res2, res2), (res2, ares2), (res2, adir1)])

    ld_acc[...] = jnp.zeros((PAD, LANES), F32)
    local_row = iota((64, LANES), 0)
    local_lane = iota((64, LANES), 1)
    slant = local_row + lax.rem(s, 2) * 64 == local_lane
    tile_of = lax.div(s, 2)

    def finish(i):
        drain(p2.at[0, i], p2_recv.at[0, i])
        drain(p2.at[1, i], p2_recv.at[1, i])
        rows = pl.ds(pl.multiple_of(s * 64, 64), 64)
        here = pl.ds(2 * i + 4 + tile_of, 1)

        def column_of(row):
            return jnp.sum(jnp.where(slant, row, 0.0), axis=1, keepdims=True)

        begin = column_of(ws[here, :])
        scale_k = column_of(rinv[here, :]) * (1.0 / samples)
        shifts = [column_of(delta[n, here, :]) * float(local) for n in range(RING)]
        lines = jnp.zeros((64, LANES), F32)
        for b in range(4):
            cols = slice(b * LANES, (b + 1) * LANES)
            low = pl.ds(2 * i + b, 1)
            high = pl.ds(2 * i + b + 4, 1)
            before = s * 64 + local_row <= b * LANES + local_lane

            def pick(ref_low, ref_high):
                return jnp.where(before, ref_low, ref_high) if b < 2 else ref_low

            if b >= 2:
                high = low
            cells = gram[i, rows, cols] + p2[0, i, :, cols] + p2[1, i, :, cols]
            for n in range(RING):
                cells = cells + shifts[n] * pick(delta[n, low, :], delta[n, high, :])
            cells = cells * (scale_k * pick(rinv[low, :], rinv[high, :]))
            cells = jnp.where(pick(spots[low, :], spots[high, :]) >= begin, cells, 0.0)
            cells = cells * cells
            lines = lines + cells
            if b >= 2:
                ld_acc[low, :] = ld_acc[low, :] + jnp.sum(cells, axis=0, keepdims=True)
            else:
                ld_acc[low, :] = ld_acc[low, :] + jnp.sum(jnp.where(before, cells, 0.0), axis=0, keepdims=True)
                ld_acc[high, :] = ld_acc[high, :] + jnp.sum(jnp.where(before, 0.0, cells), axis=0, keepdims=True)
        column = jnp.sum(lines, axis=1, keepdims=True)
        ld_acc[here, :] = ld_acc[here, :] + jnp.sum(jnp.where(slant, column, 0.0), axis=0, keepdims=True)

    def finish_side(n, carry):
        finish(n + (blocks - 4) * lax.div(n, 2))
        return carry

    def finish_centre(i, carry):
        finish(i)
        return carry

    dots_pass(2)
    rr2, inner2, cross2 = dots_end(2)
    beta1 = rr2 / rr1
    curve2 = inner2 + beta1 * (cross2 + cross2) + beta1 * beta1 * curve1
    alpha2 = rr2 / curve2
    dir2 = res2 + beta1 * dir1
    effects = alpha0 * marginal + alpha1 * dir1 + alpha2 * dir2
    eff_out[...] = effects[2 : 2 + tiles]

    lax.fori_loop(0, 4, finish_side, 0)
    sides[0] = ld_acc[0:8, :]
    sides[1] = ld_acc[16:24, :]
    trade_edges(3, sides.at[0], sides.at[1])
    lax.fori_loop(2, blocks - 2, finish_centre, 0)
    ex_x[3, s] = ld_acc[...]
    trade_ring(3)
    scores = gather_edges(3, gather_ring(3)) + diag * diag
    ld_out[...] = scores[2 : 2 + tiles]

    drain(halo_l, halo_send.at[0])
    drain(halo_r, halo_send.at[1])
    drain(st_x.at[pl.ds(0, 3)], exs_x.at[0])
    drain(st_e, exs_e.at[0])
    for e in range(4):
        drain(ex_x.at[e, pl.ds(0, 3)], exs_x.at[e + 1])
        drain(ex_e.at[e], exs_e.at[e + 1])
    for r in range(3):
        drain(red_a.at[r, pl.ds(0, near_count - 1)], sa_send.at[r])
        drain(red_b.at[r, pl.ds(0, far_count - 1)], sb_send.at[r])
    drain(gram.at[pl.ds(0, 3 * blocks // 4)], rs_send)


def shards(nvar, genotypes, phenotype, win_start, win_end):
    local, width = genotypes.shape
    near = 8 if nvar % 8 == 0 and nvar > 8 else 2
    far = nvar // near
    tiles = width // LANES
    blocks = width // WIDE
    chunks = local // LANES
    geom = (nvar, near, far, local * RING)
    vmem = pl.BlockSpec(memory_space=pltpu.VMEM)
    dma = pltpu.SemaphoreType.DMA
    effects, scores = pl.pallas_call(
        functools.partial(kernel, geom),
        out_shape=[jax.ShapeDtypeStruct((tiles, LANES), F32)] * 2,
        in_specs=[pl.BlockSpec(memory_space=pltpu.HBM)] * 3,
        out_specs=[vmem, vmem],
        scratch_shapes=[
            pltpu.VMEM((local, width), F32),
            pltpu.VMEM((local, WIDE), F32),
            pltpu.VMEM((local, WIDE), F32),
            pltpu.VMEM((local, width + 2 * WIDE), BF16),
            pltpu.VMEM((local, width + 2 * WIDE), BF16),
            pltpu.VMEM((blocks, WIDE, HALF_BAND), F32),
            pltpu.VMEM((blocks, WIDE, HALF_BAND), F32),
            pltpu.VMEM((2, blocks, 32, HALF_BAND), F32),
            pltpu.VMEM((2, blocks, 64, HALF_BAND), F32),
            pltpu.VMEM((chunks, LANES), F32),
            pltpu.VMEM((local, LANES), F32),
            pltpu.VMEM((tiles, LANES), jnp.int32),
            pltpu.VMEM((RING, 3 * PAD, LANES), F32),
            pltpu.VMEM((32, LANES), F32),
            pltpu.VMEM((32, LANES), F32),
            pltpu.VMEM((2 * RING, 32, LANES), F32),
            pltpu.VMEM((4, RING, PAD, LANES), F32),
            pltpu.VMEM((4, 2 * RING, 8, LANES), F32),
            pltpu.VMEM((3, near, 8, LANES), F32),
            pltpu.VMEM((3, far, 8, LANES), F32),
            pltpu.VMEM((RING, PAD, LANES), F32),
            pltpu.VMEM((PAD, LANES), F32),
            pltpu.VMEM((PAD, LANES), F32),
            pltpu.VMEM((PAD, LANES), F32),
            pltpu.VMEM((PAD, LANES), F32),
            pltpu.VMEM((PAD, LANES), F32),
            pltpu.VMEM((2, 8, LANES), F32),
            dma((blocks,)),
            dma((2,)),
            dma((2,)),
            dma((2,)),
            dma((5,)),
            dma((5,)),
            dma((5,)),
            dma((5,)),
            dma((3,)),
            dma((3,)),
            dma((3,)),
            dma((3,)),
            dma,
            dma((2, blocks)),
            dma((2, blocks)),
        ],
        compiler_params=pltpu.CompilerParams(
            collective_id=0, has_side_effects=True, vmem_limit_bytes=48 * 1024 * 1024
        ),
    )(genotypes, phenotype.reshape(chunks, LANES), win_start.reshape(tiles, LANES))
    return effects.reshape(width), scores.reshape(width)


def solution(mesh):
    in_specs = (P("samp", "var"), P("samp"), P("var"), P("var"))
    out_specs = (P("var"), P("var"))
    body = functools.partial(shards, mesh.shape["var"])
    return jax.shard_map(body, mesh=mesh, in_specs=in_specs, out_specs=out_specs, check_vma=False)
```

time: 83.7 us -> 69.2 us (0.83); the launches traced: 82.5 us -> 69 us
  Pallas kernels: 79.3 us -> 65.8 us
    pallas_call x1, Pallas kernels: 79.3 us -> 65.8 us  [shards(): pl.pallas_call(functools.partial(kernel, geom), out_shape=[jax.ShapeDtype...]
where the time goes in v2:
time: 69.2 us; the launch traced here: 69 us
  Pallas kernels  65.8 us (95%)
  local copies, waits for them, and re-layouts  2.58 us (4%)
    pallas_call x1, Pallas kernels, shards(): pl.pallas_call(functools.partial(kernel, geom), out_shape=[jax.ShapeDtype...  65.8 us
    unnamed x6, local copies, waits for them, and re-layouts  2.58 us

profile of v2, /device:TPU:0, one launch (start us, length us, event | category | flops | bytes accessed | tf_op | source)
XLA Modules:
  0.0 69.0 jit_solution(15412750895546459154)
XLA Ops:
  0.6 0.0 copy-start
  0.6 0.7 copy-done
  1.3 0.0 copy-start.1
  1.3 0.7 copy-done.1
  2.0 65.8 %shard_map.50 = (f32[16,128]{1,0:T(8,128)S(1)}, f32[16,128]{1,0:T(8,128)S(1)}) custom-call(f32[1024,2048]{1,0:T(8,128)} %g_hbm.1, f32[8,128]{1,0:T(8,128)S(1)} %bitcast.7, s32[16,128]{1,0:T(8,128)S(1)} %bitcast.4), custom_call_target="tpu_custom_call" | custom-call | tf_op jit(solution)/shard_map/pallas_call | solution.py:542
  67.8 0.6 copy.7
  68.4 0.6 copy.8
Async XLA Ops:
  0.6 0.7 %copy-start = (s32[2048]{0:T(1024)S(1)}, s32[2048]{0:T(1024)}, u32[]{:S(2)}) copy-start(s32[2048]{0:T(1024)} %param.6) | copy-start | bytes 24580
  1.3 0.7 copy-start.1

commit v3 on v2

--- a/solution.py
+++ b/solution.py
@@ -16,6 +16,7 @@
 LANES = 128
 WIDE = 256
 EDGE = 4
+PIECES = 4
 PAD = 24
 F32 = jnp.float32
 BF16 = jnp.bfloat16
@@ -32,12 +33,12 @@
     eff_out, ld_out,
     g_v, halo_l, halo_r, xh, xl, gram, band, p1, p2,
     phen, phcol, ws_in,
-    st_x, st_l, st_r, st_e, ex_x, ex_e, red_a, red_b,
-    delta, rinv, ws, spots, vec, ld_acc, sides,
+    st_x, st_l, st_r, st_e, ex_x, ex_e, red, acc,
+    delta, rinv, ws, spots, vec, ld_acc, sides, centres,
     load_sem, small_sem, halo_send, halo_recv, exs_x, exr_x, exs_e, exr_e,
-    sa_send, sa_recv, sb_send, sb_recv, rs_send, p1_recv, p2_recv,
+    red_send, red_recv, rs_send, p1_recv, p2_recv,
 ):
-    nvar, near_count, far_count, samples = geom
+    nvar, samples = geom
     tiles = ws_in.shape[0]
     width = tiles * LANES
     variants = nvar * width
@@ -46,8 +47,6 @@
     chunks = local // LANES
     s = lax.axis_index("samp")
     d = lax.axis_index("var")
-    near = lax.rem(d, near_count)
-    far = lax.div(d, near_count)
 
     def samp_at(step):
         return lax.rem(s + step, RING)
@@ -61,9 +60,8 @@
     ring_peers = [dev(samp_at(i), d) for i in range(1, RING)]
     right_edge = [dev(samp_at(i), var_at(1)) for i in range(RING)]
     left_edge = [dev(samp_at(i), var_at(-1)) for i in range(RING)]
-    near_peers = [dev(s, far * near_count + lax.rem(near + i, near_count)) for i in range(1, near_count)]
-    far_peers = [dev(s, lax.rem(far + i, far_count) * near_count + near) for i in range(1, far_count)]
-    greeted = ring_peers + right_edge + left_edge + near_peers + far_peers
+    var_peers = [dev(s, var_at(i)) for i in range(1, nvar)]
+    greeted = ring_peers + right_edge[1:] + left_edge[1:] + var_peers
 
     def remote(src, dst, send, recv, device):
         copy = pltpu.make_async_remote_copy(
@@ -112,7 +110,7 @@
     ws[...] = jnp.zeros((PAD, LANES), F32)
     ws[2 : 2 + tiles, :] = ws_in[...].astype(F32)
 
-    def prepare(source, lane, group, keep):
+    def prepare(source, lane, group):
         def rows_of(c):
             return pl.ds(pl.multiple_of(c * LANES, LANES), LANES)
 
@@ -133,62 +131,36 @@
                 top = off.astype(BF16)
                 xh[rows, goal] = top
                 xl[rows, goal] = (off - top.astype(F32)).astype(BF16)
-                if keep:
-                    sq = sq + jnp.sum((off * off).reshape(LANES // 8, 8, LANES), axis=0)
-                    pp = pp + jnp.sum((off * phcol[rows, :]).reshape(LANES // 8, 8, LANES), axis=0)
+                sq = sq + jnp.sum((off * off).reshape(LANES // 8, 8, LANES), axis=0)
+                pp = pp + jnp.sum((off * phcol[rows, :]).reshape(LANES // 8, 8, LANES), axis=0)
                 return sq, pp
 
             start = (jnp.zeros((8, LANES), F32), jnp.zeros((8, LANES), F32))
-            sq, pp = lax.fori_loop(0, chunks, split, start)
-            if keep:
-                line = 2 * group + h
-                mine[pl.ds(line, 1), :] = centre
-                mine[pl.ds(PAD + line, 1), :] = jnp.sum(sq, axis=0, keepdims=True)
-                mine[pl.ds(2 * PAD + line, 1), :] = jnp.sum(pp, axis=0, keepdims=True)
-
-    def prepare_own(group, carry):
-        load(group).wait()
-        prepare(g_v, pl.multiple_of((group - 1) * WIDE, WIDE), group, True)
-        return carry
-
-    lax.fori_loop(1, blocks + 1, prepare_own, 0)
-    mine[2 * PAD + tiles + 4 : 2 * PAD + tiles + 5, :] = jnp.broadcast_to(own_phi, (1, LANES))
-    for k in range(3):
-        st_l[8 * k : 8 * k + 8, :] = mine[PAD * k : PAD * k + 8, :]
-        st_r[8 * k : 8 * k + 8, :] = mine[PAD * k + 16 : PAD * k + 24, :]
-    st_l[24:32, :] = ws[0:8, :]
-    st_r[24:32, :] = ws[16:24, :]
-
-    pl.semaphore_wait(barrier, len(greeted))
-    remote(g_hbm.at[:, pl.ds(width - WIDE, WIDE)], halo_l, halo_send.at[0], halo_recv.at[0], dev(s, var_at(1)))
-    remote(g_hbm.at[:, pl.ds(0, WIDE)], halo_r, halo_send.at[1], halo_recv.at[1], dev(s, var_at(-1)))
-    for peer in ring_peers:
-        remote(st_x.at[s], st_x.at[s], exs_x.at[0], exr_x.at[0], peer)
-    for i in range(RING):
-        remote(st_r, st_e.at[s], exs_e.at[0], exr_e.at[0], right_edge[i])
-    for i in range(RING):
-        remote(st_l, st_e.at[RING + s], exs_e.at[0], exr_e.at[0], left_edge[i])
+            sq, pp = lax.fori_loop(0, chunks, split, start, unroll=True)
+            line = 2 * group + h
+            mine[pl.ds(line, 1), :] = centre
+            mine[pl.ds(PAD + line, 1), :] = jnp.sum(sq, axis=0, keepdims=True)
+            mine[pl.ds(2 * PAD + line, 1), :] = jnp.sum(pp, axis=0, keepdims=True)
 
     wrap = iota((WIDE, WIDE), 0) > iota((WIDE, WIDE), 1)
 
+    def product(left, right, rows):
+        def part(ref, group):
+            return ref[rows, pl.ds(pl.multiple_of(group * WIDE, WIDE), WIDE)]
+
+        dims = (((0,), (0,)), ((), ()))
+        left_h, left_l = part(xh, left), part(xl, left)
+        right_h, right_l = part(xh, right), part(xl, right)
+        return (
+            lax.dot_general(left_h, right_h, dims, preferred_element_type=F32)
+            + lax.dot_general(left_h, right_l, dims, preferred_element_type=F32)
+            + lax.dot_general(left_l, right_h, dims, preferred_element_type=F32)
+        )
+
     def gram_block(i):
-        pick = pl.ds(pl.multiple_of((i + 2) * WIDE, WIDE), WIDE)
-        row_h = xh[:, pick].T
-        row_l = xl[:, pick].T
-
-        def product(t):
-            near_pick = pl.ds(pl.multiple_of((i + t) * WIDE, WIDE), WIDE)
-            col_h = xh[:, near_pick]
-            col_l = xl[:, near_pick]
-            dims = (((1,), (0,)), ((), ()))
-            return (
-                lax.dot_general(row_h, col_h, dims, preferred_element_type=F32)
-                + lax.dot_general(row_h, col_l, dims, preferred_element_type=F32)
-                + lax.dot_general(row_l, col_h, dims, preferred_element_type=F32)
-            )
-
-        gram[i, :, 0:WIDE] = jnp.where(wrap, product(2), product(0))
-        gram[i, :, WIDE:HALF_BAND] = product(1)
+        whole = pl.ds(0, local)
+        gram[i, :, 0:WIDE] = jnp.where(wrap, product(i + 2, i + 2, whole), product(i + 2, i, whole))
+        gram[i, :, WIDE:HALF_BAND] = product(i + 2, i + 1, whole)
 
     half = 32
     ahead = samp_at(1)
@@ -214,6 +186,41 @@
         p1[1, i] = p1[1, i] + gram[i, pl.ds(pl.multiple_of(behind * 64 + half, half), half), :]
         remote(p1.at[1, i], p2.at[1, i, pl.ds(half, half), :], rs_send, p2_recv.at[1, i], dev(behind, d))
 
+    def prepare_own(group, carry):
+        load(group).wait()
+        prepare(g_v, pl.multiple_of((group - 1) * WIDE, WIDE), group)
+        return carry
+
+    lax.fori_loop(1, 4, prepare_own, 0)
+    pl.semaphore_wait(barrier, len(greeted))
+    for c in range(PIECES):
+        rows = pl.ds(c * (local // PIECES), local // PIECES)
+        for side, device, cols, goal in (
+            (0, dev(s, var_at(1)), pl.ds(width - WIDE, WIDE), halo_l),
+            (1, dev(s, var_at(-1)), pl.ds(0, WIDE), halo_r),
+        ):
+            remote(g_hbm.at[rows, cols], goal.at[rows], halo_send.at[side], halo_recv.at[side, c], device)
+    gram_block(1)
+    send_far(1)
+    send_direct(1)
+    lax.fori_loop(4, blocks + 1, prepare_own, 0)
+    mine[2 * PAD + tiles + 4 : 2 * PAD + tiles + 5, :] = jnp.broadcast_to(own_phi, (1, LANES))
+    for k in range(3):
+        st_l[8 * k : 8 * k + 8, :] = mine[PAD * k : PAD * k + 8, :]
+        st_r[8 * k : 8 * k + 8, :] = mine[PAD * k + 16 : PAD * k + 24, :]
+    st_l[24:32, :] = ws[0:8, :]
+    st_r[24:32, :] = ws[16:24, :]
+
+    for peer in ring_peers:
+        remote(st_x.at[s], st_x.at[s], exs_x.at[0], exr_x.at[0], peer)
+    for i in range(RING):
+        remote(st_r, st_e.at[s], exs_e.at[0], exr_e.at[0], right_edge[i])
+    for i in range(RING):
+        remote(st_l, st_e.at[RING + s], exs_e.at[0], exr_e.at[0], left_edge[i])
+
+    gram[0, :, 0:WIDE] = product(2, 2, pl.ds(0, local))
+    gram[0, :, WIDE:HALF_BAND] = product(2, 1, pl.ds(0, local))
+
     def inner(i, carry):
         gram_block(i)
         send_far(i)
@@ -224,7 +231,7 @@
 
         return carry
 
-    lax.fori_loop(1, blocks - 1, inner, 0)
+    lax.fori_loop(2, blocks - 1, inner, 0)
 
     grid_row = iota((PAD, LANES), 0)
     place = d * width - WIDE + grid_row * LANES + iota((PAD, LANES), 1)
@@ -260,6 +267,7 @@
     spread = total * (1.0 / samples)
     scale = lax.rsqrt(spread + EPS)
     rinv[...] = scale
+    centres[...] = stat(0, s)
     spots[...] = place.astype(F32)
     marginal = jnp.where(inside, joint * scale * (1.0 / math.sqrt(samples)), 0.0)
     diag = jnp.where(inside, spread * (scale * scale), 0.0)
@@ -355,24 +363,13 @@
     def dots_send(r, pairs):
         rows = [jnp.sum(jnp.where(own, a * b, 0.0), axis=0, keepdims=True) for a, b in pairs]
         rows.append(jnp.zeros((8 - len(rows), LANES), F32))
-        red_a[r, near] = jnp.concatenate(rows, axis=0)
-        for peer in near_peers:
-            remote(red_a.at[r, near], red_a.at[r, near], sa_send.at[r], sa_recv.at[r], peer)
-
-    def dots_pass(r):
-        drain(red_a.at[r, pl.ds(0, near_count - 1)], sa_recv.at[r])
-        total = red_a[r, 0]
-        for i in range(1, near_count):
-            total = total + red_a[r, i]
-        red_b[r, far] = total
-        for peer in far_peers:
-            remote(red_b.at[r, far], red_b.at[r, far], sb_send.at[r], sb_recv.at[r], peer)
+        red[r, d] = jnp.concatenate(rows, axis=0)
+        for peer in var_peers:
+            remote(red.at[r, d], red.at[r, d], red_send.at[r], red_recv.at[r], peer)
 
     def dots_end(r):
-        drain(red_b.at[r, pl.ds(0, far_count - 1)], sb_recv.at[r])
-        total = red_b[r, 0]
-        for i in range(1, far_count):
-            total = total + red_b[r, i]
+        drain(red.at[r, pl.ds(0, nvar - 1)], red_recv.at[r])
+        total = jnp.sum(red[r], axis=0)
         sums = jnp.broadcast_to(jnp.sum(total, axis=1, keepdims=True), (8, LANES))
         return [sums[k : k + 1] for k in range(3)]
 
@@ -381,12 +378,27 @@
 
     vec[...] = scale * marginal
     apply_centre(0)
-    drain(halo_l, halo_recv.at[0])
-    prepare(halo_l, 0, 0, False)
-    gram_block(0)
-    drain(halo_r, halo_recv.at[1])
-    prepare(halo_r, 0, blocks + 1, False)
-    gram_block(blocks - 1)
+    def halo_piece(c, carry):
+        size = local // PIECES
+        rows = pl.ds(pl.multiple_of(c * size, size), size)
+        for side, source, group in ((0, halo_l, 0), (1, halo_r, blocks + 1)):
+            drain(source.at[rows], halo_recv.at[side, c])
+            for h in range(2):
+                off = source[rows, h * LANES : (h + 1) * LANES] - centres[2 * group + h : 2 * group + h + 1, :]
+                top = off.astype(BF16)
+                cols = slice(group * WIDE + h * LANES, group * WIDE + (h + 1) * LANES)
+                xh[rows, cols] = top
+                xl[rows, cols] = (off - top.astype(F32)).astype(BF16)
+        last = blocks + 1
+        for k, pair in enumerate(((2, 0), (last, last - 2), (last, last - 1), (last, last))):
+            acc[k] = acc[k] + product(pair[0], pair[1], rows)
+        return carry
+
+    acc[...] = jnp.zeros_like(acc)
+    lax.fori_loop(0, PIECES, halo_piece, 0)
+    gram[0, :, 0:WIDE] = jnp.where(wrap, gram[0, :, 0:WIDE], acc[0])
+    gram[blocks - 1, :, 0:WIDE] = jnp.where(wrap, acc[3], acc[1])
+    gram[blocks - 1, :, WIDE:HALF_BAND] = acc[2]
     mask_block(0)
     mask_block(blocks - 1)
     apply_sides(0)
@@ -409,8 +421,7 @@
     relay(blocks - 2)
     relay(0)
     relay(blocks - 1)
-    send_direct(1)
-    dots_pass(0)
+    send_direct(blocks - 2)
 
     part = gather_ring(1)
     vec[...] = scale * (outer * part + weight * image0)
@@ -420,7 +431,7 @@
     apply_sides(2)
     trade_edges(2)
     trade_ring(2)
-    for i in (blocks - 2, 0, blocks - 1):
+    for i in (0, blocks - 1):
         send_direct(i)
     for i in range(2, blocks - 2):
         send_direct(i)
@@ -429,7 +440,6 @@
     res1 = marginal - alpha0 * image0
     ares1 = image0 - alpha0 * image1
     dots_send(1, [(res1, res1), (res1, ares1), (res1, image0)])
-    dots_pass(1)
 
     part = gather_ring(2)
     image2 = outer * gather_edges(2, part) + weight * image1
@@ -497,7 +507,6 @@
         finish(i)
         return carry
 
-    dots_pass(2)
     rr2, inner2, cross2 = dots_end(2)
     beta1 = rr2 / rr1
     curve2 = inner2 + beta1 * (cross2 + cross2) + beta1 * beta1 * curve1
@@ -524,19 +533,16 @@
         drain(ex_x.at[e, pl.ds(0, 3)], exs_x.at[e + 1])
         drain(ex_e.at[e], exs_e.at[e + 1])
     for r in range(3):
-        drain(red_a.at[r, pl.ds(0, near_count - 1)], sa_send.at[r])
-        drain(red_b.at[r, pl.ds(0, far_count - 1)], sb_send.at[r])
+        drain(red.at[r, pl.ds(0, nvar - 1)], red_send.at[r])
     drain(gram.at[pl.ds(0, 3 * blocks // 4)], rs_send)
 
 
 def shards(nvar, genotypes, phenotype, win_start, win_end):
     local, width = genotypes.shape
-    near = 8 if nvar % 8 == 0 and nvar > 8 else 2
-    far = nvar // near
     tiles = width // LANES
     blocks = width // WIDE
     chunks = local // LANES
-    geom = (nvar, near, far, local * RING)
+    geom = (nvar, local * RING)
     vmem = pl.BlockSpec(memory_space=pltpu.VMEM)
     dma = pltpu.SemaphoreType.DMA
     effects, scores = pl.pallas_call(
@@ -563,8 +569,8 @@
             pltpu.VMEM((2 * RING, 32, LANES), F32),
             pltpu.VMEM((4, RING, PAD, LANES), F32),
             pltpu.VMEM((4, 2 * RING, 8, LANES), F32),
-            pltpu.VMEM((3, near, 8, LANES), F32),
-            pltpu.VMEM((3, far, 8, LANES), F32),
+            pltpu.VMEM((3, nvar, 8, LANES), F32),
+            pltpu.VMEM((4, WIDE, WIDE), F32),
             pltpu.VMEM((RING, PAD, LANES), F32),
             pltpu.VMEM((PAD, LANES), F32),
             pltpu.VMEM((PAD, LANES), F32),
@@ -572,16 +578,15 @@
             pltpu.VMEM((PAD, LANES), F32),
             pltpu.VMEM((PAD, LANES), F32),
             pltpu.VMEM((2, 8, LANES), F32),
+            pltpu.VMEM((PAD, LANES), F32),
             dma((blocks,)),
             dma((2,)),
             dma((2,)),
-            dma((2,)),
+            dma((2, PIECES)),
             dma((5,)),
             dma((5,)),
             dma((5,)),
             dma((5,)),
-            dma((3,)),
-            dma((3,)),
             dma((3,)),
             dma((3,)),
             dma,

time: 69.2 us -> 63.4 us (0.916)
  Pallas kernels: 65.8 us -> 59.8 us
    pallas_call x1, Pallas kernels: 65.8 us -> 59.8 us  [shards(): pl.pallas_call(functools.partial(kernel, geom), out_shape=[jax.ShapeDtype...]
where the time goes in v3:
time: 63.4 us; the launch traced here: 63 us
  Pallas kernels  59.8 us (94%)
  local copies, waits for them, and re-layouts  2.58 us (4%)
  between operations  0.65 us (1%)
    pallas_call x1, Pallas kernels, shards(): pl.pallas_call(functools.partial(kernel, geom), out_shape=[jax.ShapeDtype...  59.8 us
    unnamed x6, local copies, waits for them, and re-layouts  2.58 us

profile of v3, /device:TPU:0, one launch (start us, length us, event | category | flops | bytes accessed | tf_op | source)
XLA Modules:
  0.0 63.0 jit_solution(17653383004099064090)
XLA Ops:
  0.6 0.0 copy-start
  0.6 0.7 %copy-done = s32[2048]{0:T(1024)S(1)} copy-done((s32[2048]{0:T(1024)S(1)}, s32[2048]{0:T(1024)}, u32[]{:S(2)}) %copy-start) | copy-done | bytes 8216
  1.3 0.0 copy-start.1
  1.3 0.7 %copy-done.1 = f32[1024]{0:T(1024)S(1)} copy-done((f32[1024]{0:T(1024)S(1)}, f32[1024]{0:T(1024)}, u32[]{:S(2)}) %copy-start.1) | copy-done | bytes 4120
  2.0 59.8 %shard_map.50 = (f32[16,128]{1,0:T(8,128)S(1)}, f32[16,128]{1,0:T(8,128)S(1)}) custom-call(f32[1024,2048]{1,0:T(8,128)} %g_hbm.1, f32[8,128]{1,0:T(8,128)S(1)} %bitcast.7, s32[16,128]{1,0:T(8,128)S(1)} %bitcast.4), custom_call_target="tpu_custom_call" | custom-call | tf_op jit(solution)/shard_map/pallas_call | solution.py:548
  61.8 0.6 copy.7
  62.4 0.6 copy.8
Async XLA Ops:
  0.6 0.7 %copy-start = (s32[2048]{0:T(1024)S(1)}, s32[2048]{0:T(1024)}, u32[]{:S(2)}) copy-start(s32[2048]{0:T(1024)} %param.6) | copy-start | bytes 24580
  1.3 0.7 %copy-start.1 = (f32[1024]{0:T(1024)S(1)}, f32[1024]{0:T(1024)}, u32[]{:S(2)}) copy-start(f32[1024]{0:T(1024)} %param.5) | copy-start | bytes 12292

commit v4 on v3

--- a/solution.py
+++ b/solution.py
@@ -36,9 +36,9 @@
     st_x, st_l, st_r, st_e, ex_x, ex_e, red, acc,
     delta, rinv, ws, spots, vec, ld_acc, sides, centres,
     load_sem, small_sem, halo_send, halo_recv, exs_x, exr_x, exs_e, exr_e,
-    red_send, red_recv, rs_send, p1_recv, p2_recv,
+    red_send, red_recv, ready, known, rs_send, p1_recv, p2_recv,
 ):
-    nvar, samples = geom
+    nvar, near_count, far_count, samples = geom
     tiles = ws_in.shape[0]
     width = tiles * LANES
     variants = nvar * width
@@ -48,6 +48,9 @@
     s = lax.axis_index("samp")
     d = lax.axis_index("var")
 
+    near = lax.rem(d, near_count)
+    far = lax.div(d, near_count)
+
     def samp_at(step):
         return lax.rem(s + step, RING)
 
@@ -61,7 +64,9 @@
     right_edge = [dev(samp_at(i), var_at(1)) for i in range(RING)]
     left_edge = [dev(samp_at(i), var_at(-1)) for i in range(RING)]
     var_peers = [dev(s, var_at(i)) for i in range(1, nvar)]
-    greeted = ring_peers + right_edge[1:] + left_edge[1:] + var_peers
+    near_peers = [dev(s, far * near_count + lax.rem(near + i, near_count)) for i in range(1, near_count)]
+    far_peers = [dev(s, lax.rem(far + i, far_count) * near_count + near) for i in range(1, far_count)]
+    greeted = ring_peers + right_edge[:1] + left_edge[:1] + near_peers + far_peers
 
     def remote(src, dst, send, recv, device):
         copy = pltpu.make_async_remote_copy(
@@ -111,42 +116,34 @@
     ws[2 : 2 + tiles, :] = ws_in[...].astype(F32)
 
     def prepare(source, lane, group):
-        def rows_of(c):
-            return pl.ds(pl.multiple_of(c * LANES, LANES), LANES)
-
         for h in range(2):
-            cols = pl.ds(pl.multiple_of(lane + h * LANES, LANES), LANES)
-            goal = pl.ds(pl.multiple_of(group * WIDE + h * LANES, LANES), LANES)
-
-            def add(c, total):
-                return total + jnp.sum(source[rows_of(c), cols].reshape(LANES // 8, 8, LANES), axis=0)
-
-            total = lax.fori_loop(0, chunks, add, jnp.zeros((8, LANES), F32), unroll=True)
+            cols = slice(lane + h * LANES, lane + (h + 1) * LANES)
+            goal = slice(group * WIDE + h * LANES, group * WIDE + (h + 1) * LANES)
+            total = jnp.zeros((8, LANES), F32)
+            for c in range(chunks):
+                values = source[c * LANES : (c + 1) * LANES, cols]
+                total = total + jnp.sum(values.reshape(LANES // 8, 8, LANES), axis=0)
             centre = jnp.sum(total, axis=0, keepdims=True) * (1.0 / local)
-
-            def split(c, carry):
-                sq, pp = carry
-                rows = rows_of(c)
+            sq = jnp.zeros((8, LANES), F32)
+            pp = jnp.zeros((8, LANES), F32)
+            for c in range(chunks):
+                rows = slice(c * LANES, (c + 1) * LANES)
                 off = source[rows, cols] - centre
                 top = off.astype(BF16)
                 xh[rows, goal] = top
                 xl[rows, goal] = (off - top.astype(F32)).astype(BF16)
                 sq = sq + jnp.sum((off * off).reshape(LANES // 8, 8, LANES), axis=0)
                 pp = pp + jnp.sum((off * phcol[rows, :]).reshape(LANES // 8, 8, LANES), axis=0)
-                return sq, pp
-
-            start = (jnp.zeros((8, LANES), F32), jnp.zeros((8, LANES), F32))
-            sq, pp = lax.fori_loop(0, chunks, split, start, unroll=True)
             line = 2 * group + h
-            mine[pl.ds(line, 1), :] = centre
-            mine[pl.ds(PAD + line, 1), :] = jnp.sum(sq, axis=0, keepdims=True)
-            mine[pl.ds(2 * PAD + line, 1), :] = jnp.sum(pp, axis=0, keepdims=True)
+            mine[line : line + 1, :] = centre
+            mine[PAD + line : PAD + line + 1, :] = jnp.sum(sq, axis=0, keepdims=True)
+            mine[2 * PAD + line : 2 * PAD + line + 1, :] = jnp.sum(pp, axis=0, keepdims=True)
 
     wrap = iota((WIDE, WIDE), 0) > iota((WIDE, WIDE), 1)
 
     def product(left, right, rows):
         def part(ref, group):
-            return ref[rows, pl.ds(pl.multiple_of(group * WIDE, WIDE), WIDE)]
+            return ref[rows, pl.ds(group * WIDE, WIDE)]
 
         dims = (((0,), (0,)), ((), ()))
         left_h, left_l = part(xh, left), part(xl, left)
@@ -186,24 +183,41 @@
         p1[1, i] = p1[1, i] + gram[i, pl.ds(pl.multiple_of(behind * 64 + half, half), half), :]
         remote(p1.at[1, i], p2.at[1, i, pl.ds(half, half), :], rs_send, p2_recv.at[1, i], dev(behind, d))
 
-    def prepare_own(group, carry):
+    def prepare_own(*groups):
+        for group in groups:
+            prepare(g_v, (group - 1) * WIDE, group)
+
+    for group in range(1, 4):
         load(group).wait()
-        prepare(g_v, pl.multiple_of((group - 1) * WIDE, WIDE), group)
-        return carry
-
-    lax.fori_loop(1, 4, prepare_own, 0)
+        prepare_own(group)
     pl.semaphore_wait(barrier, len(greeted))
-    for c in range(PIECES):
+    for peer in ring_peers:
+        pl.semaphore_signal(ready, inc=1, device_id=peer, device_id_type=MESH)
+    for peer in near_peers:
+        pl.semaphore_signal(known, inc=1, device_id=peer, device_id_type=MESH)
+
+    def send_halo(c):
         rows = pl.ds(c * (local // PIECES), local // PIECES)
         for side, device, cols, goal in (
             (0, dev(s, var_at(1)), pl.ds(width - WIDE, WIDE), halo_l),
             (1, dev(s, var_at(-1)), pl.ds(0, WIDE), halo_r),
         ):
             remote(g_hbm.at[rows, cols], goal.at[rows], halo_send.at[side], halo_recv.at[side, c], device)
+
+    send_halo(0)
+    send_halo(1)
+    for group in range(4, blocks + 1):
+        load(group).wait()
     gram_block(1)
     send_far(1)
     send_direct(1)
-    lax.fori_loop(4, blocks + 1, prepare_own, 0)
+    prepare_own(4)
+    gram_block(2)
+    prepare_own(5, 6)
+    send_far(2)
+    prepare_own(7)
+    gram_block(3)
+    prepare_own(*range(8, blocks + 1))
     mine[2 * PAD + tiles + 4 : 2 * PAD + tiles + 5, :] = jnp.broadcast_to(own_phi, (1, LANES))
     for k in range(3):
         st_l[8 * k : 8 * k + 8, :] = mine[PAD * k : PAD * k + 8, :]
@@ -213,25 +227,29 @@
 
     for peer in ring_peers:
         remote(st_x.at[s], st_x.at[s], exs_x.at[0], exr_x.at[0], peer)
+    send_far(3)
+    pl.semaphore_wait(ready, RING - 1)
     for i in range(RING):
         remote(st_r, st_e.at[s], exs_e.at[0], exr_e.at[0], right_edge[i])
     for i in range(RING):
         remote(st_l, st_e.at[RING + s], exs_e.at[0], exr_e.at[0], left_edge[i])
-
-    gram[0, :, 0:WIDE] = product(2, 2, pl.ds(0, local))
-    gram[0, :, WIDE:HALF_BAND] = product(2, 1, pl.ds(0, local))
-
-    def inner(i, carry):
+    for c in range(2, PIECES):
+        send_halo(c)
+
+    whole = pl.ds(0, local)
+    gram[0, :, 0:WIDE] = product(2, 2, whole)
+    gram[0, :, WIDE:HALF_BAND] = product(2, 1, whole)
+    gram_block(4)
+    send_far(4)
+    relay(1)
+    for i in range(5, blocks - 1):
         gram_block(i)
         send_far(i)
-
-        @pl.when(i >= 5)
-        def _():
-            relay(i - 4)
-
-        return carry
-
-    lax.fori_loop(2, blocks - 1, inner, 0)
+        if i == 5:
+            relay(2)
+    send_direct(2)
+    send_direct(3)
+    relay(3)
 
     grid_row = iota((PAD, LANES), 0)
     place = d * width - WIDE + grid_row * LANES + iota((PAD, LANES), 1)
@@ -406,7 +424,7 @@
     trade_ring(0)
     send_far(0)
     send_far(blocks - 1)
-    for i in range(3, blocks - 2):
+    for i in range(4, blocks - 2):
         relay(i)
 
     part = gather_ring(0)
@@ -417,6 +435,7 @@
     apply_sides(1)
     trade_edges(1)
     trade_ring(1)
+    pl.semaphore_wait(known, near_count - 1)
     dots_send(0, [(marginal, marginal), (marginal, image0)])
     relay(blocks - 2)
     relay(0)
@@ -433,7 +452,7 @@
     trade_ring(2)
     for i in (0, blocks - 1):
         send_direct(i)
-    for i in range(2, blocks - 2):
+    for i in range(4, blocks - 2):
         send_direct(i)
     rr0, curve0 = dots_end(0)[:2]
     alpha0 = rr0 / curve0
@@ -507,6 +526,13 @@
         finish(i)
         return carry
 
+    lax.fori_loop(0, 4, finish_side, 0)
+    sides[0] = ld_acc[0:8, :]
+    sides[1] = ld_acc[16:24, :]
+    trade_edges(3, sides.at[0], sides.at[1])
+    lax.fori_loop(2, blocks - 2, finish_centre, 0)
+    ex_x[3, s] = ld_acc[...]
+    trade_ring(3)
     rr2, inner2, cross2 = dots_end(2)
     beta1 = rr2 / rr1
     curve2 = inner2 + beta1 * (cross2 + cross2) + beta1 * beta1 * curve1
@@ -515,13 +541,6 @@
     effects = alpha0 * marginal + alpha1 * dir1 + alpha2 * dir2
     eff_out[...] = effects[2 : 2 + tiles]
 
-    lax.fori_loop(0, 4, finish_side, 0)
-    sides[0] = ld_acc[0:8, :]
-    sides[1] = ld_acc[16:24, :]
-    trade_edges(3, sides.at[0], sides.at[1])
-    lax.fori_loop(2, blocks - 2, finish_centre, 0)
-    ex_x[3, s] = ld_acc[...]
-    trade_ring(3)
     scores = gather_edges(3, gather_ring(3)) + diag * diag
     ld_out[...] = scores[2 : 2 + tiles]
 
@@ -542,7 +561,9 @@
     tiles = width // LANES
     blocks = width // WIDE
     chunks = local // LANES
-    geom = (nvar, local * RING)
+    near = 8 if nvar % 8 == 0 and nvar > 8 else 2
+    far = nvar // near
+    geom = (nvar, near, far, local * RING)
     vmem = pl.BlockSpec(memory_space=pltpu.VMEM)
     dma = pltpu.SemaphoreType.DMA
     effects, scores = pl.pallas_call(
@@ -589,6 +610,8 @@
             dma((5,)),
             dma((3,)),
             dma((3,)),
+            pltpu.SemaphoreType.REGULAR,
+            pltpu.SemaphoreType.REGULAR,
             dma,
             dma((2, blocks)),
             dma((2, blocks)),

time: 63.4 us -> 59 us (0.931)
  Pallas kernels: 59.8 us -> 55.6 us
    pallas_call x1, Pallas kernels: 59.8 us -> 55.6 us  [shards(): pl.pallas_call(functools.partial(kernel, geom), out_shape=[jax.ShapeDtype...]
where the time goes in v4:
time: 59 us; the launch traced here: 58.8 us
  Pallas kernels  55.6 us (94%)
  local copies, waits for them, and re-layouts  2.58 us (4%)
  between operations  0.65 us (1%)
    pallas_call x1, Pallas kernels, shards(): pl.pallas_call(functools.partial(kernel, geom), out_shape=[jax.ShapeDtype...  55.6 us
    unnamed x6, local copies, waits for them, and re-layouts  2.58 us

profile of v4, /device:TPU:0, one launch (start us, length us, event | category | flops | bytes accessed | tf_op | source)
XLA Modules:
  0.0 58.8 jit_solution(6036712225696914774)
XLA Ops:
  0.6 0.0 copy-start
  0.6 0.7 %copy-done = s32[2048]{0:T(1024)S(1)} copy-done((s32[2048]{0:T(1024)S(1)}, s32[2048]{0:T(1024)}, u32[]{:S(2)}) %copy-start) | copy-done | bytes 8216
  1.3 0.0 copy-start.1
  1.3 0.7 %copy-done.1 = f32[1024]{0:T(1024)S(1)} copy-done((f32[1024]{0:T(1024)S(1)}, f32[1024]{0:T(1024)}, u32[]{:S(2)}) %copy-start.1) | copy-done | bytes 4120
  2.0 55.6 %shard_map.50 = (f32[16,128]{1,0:T(8,128)S(1)}, f32[16,128]{1,0:T(8,128)S(1)}) custom-call(f32[1024,2048]{1,0:T(8,128)} %g_hbm.1, f32[8,128]{1,0:T(8,128)S(1)} %bitcast.7, s32[16,128]{1,0:T(8,128)S(1)} %bitcast.4), custom_call_target="tpu_custom_call" | custom-call | tf_op jit(solution)/shard_map/pallas_call | solution.py:569
  57.6 0.6 %copy.7 = f32[2048]{0:T(1024)} copy(f32[2048]{0:T(1024)S(1)} %bitcast.6) | data formatting | bytes 16384
  58.2 0.6 %copy.8 = f32[2048]{0:T(1024)} copy(f32[2048]{0:T(1024)S(1)} %bitcast.5) | data formatting | bytes 16384
Async XLA Ops:
  0.6 0.7 %copy-start = (s32[2048]{0:T(1024)S(1)}, s32[2048]{0:T(1024)}, u32[]{:S(2)}) copy-start(s32[2048]{0:T(1024)} %param.6) | copy-start | bytes 24580
  1.3 0.7 %copy-start.1 = (f32[1024]{0:T(1024)S(1)}, f32[1024]{0:T(1024)}, u32[]{:S(2)}) copy-start(f32[1024]{0:T(1024)} %param.5) | copy-start | bytes 12292

commit v5 on v4

--- a/solution.py
+++ b/solution.py
@@ -30,7 +30,7 @@
 def kernel(
     geom,
     g_hbm, phen_hbm, ws_hbm,
-    eff_out, ld_out,
+    out,
     g_v, halo_l, halo_r, xh, xl, gram, band, p1, p2,
     phen, phcol, ws_in,
     st_x, st_l, st_r, st_e, ex_x, ex_e, red, acc,
@@ -220,10 +220,10 @@
     prepare_own(*range(8, blocks + 1))
     mine[2 * PAD + tiles + 4 : 2 * PAD + tiles + 5, :] = jnp.broadcast_to(own_phi, (1, LANES))
     for k in range(3):
-        st_l[8 * k : 8 * k + 8, :] = mine[PAD * k : PAD * k + 8, :]
-        st_r[8 * k : 8 * k + 8, :] = mine[PAD * k + 16 : PAD * k + 24, :]
-    st_l[24:32, :] = ws[0:8, :]
-    st_r[24:32, :] = ws[16:24, :]
+        st_l[EDGE * k : EDGE * (k + 1), :] = mine[PAD * k : PAD * k + EDGE, :]
+        st_r[EDGE * k : EDGE * (k + 1), :] = mine[PAD * k + 16 : PAD * k + 16 + EDGE, :]
+    st_l[3 * EDGE : 4 * EDGE, :] = ws[0:EDGE, :]
+    st_r[3 * EDGE : 4 * EDGE, :] = ws[16 : 16 + EDGE, :]
 
     for peer in ring_peers:
         remote(st_x.at[s], st_x.at[s], exs_x.at[0], exr_x.at[0], peer)
@@ -265,11 +265,14 @@
     drain(st_x.at[pl.ds(0, 3)], exr_x.at[0])
     drain(st_e, exr_e.at[0])
 
+    def padded(rows):
+        return jnp.concatenate([rows, jnp.zeros((8 - EDGE, LANES), F32)], axis=0)
+
     def stat(k, i):
         return extend(
             st_x[i, PAD * k : PAD * (k + 1), :],
-            st_e[i, 8 * k : 8 * k + 8, :],
-            st_e[RING + i, 8 * k : 8 * k + 8, :],
+            padded(st_e[i, EDGE * k : EDGE * (k + 1), :]),
+            padded(st_e[RING + i, EDGE * k : EDGE * (k + 1), :]),
         )
 
     means = [stat(0, i) for i in range(RING)]
@@ -289,7 +292,7 @@
     spots[...] = place.astype(F32)
     marginal = jnp.where(inside, joint * scale * (1.0 / math.sqrt(samples)), 0.0)
     diag = jnp.where(inside, spread * (scale * scale), 0.0)
-    ws_bottom = ws[16:24, :] + jnp.where(edge_rows, st_e[RING, 24:32, :], 0.0)
+    ws_bottom = ws[16:24, :] + padded(st_e[RING, 3 * EDGE : 4 * EDGE, :])
     ws[16:24, :] = ws_bottom + jnp.where(place[16:24] >= variants, F32(variants), 0.0)
 
     def mask_block(i):
@@ -318,7 +321,7 @@
     lax.fori_loop(1, blocks - 1, mask_inner, 0)
 
     def apply_block(e, i):
-        out = ex_x.at[e, s]
+        part = ex_x.at[e, s]
         for a in range(2):
             here = pl.ds(2 * i + 4 + a, 1)
             column = to_column(vec[here, :])
@@ -330,15 +333,15 @@
                 moved = cells * column
                 if b >= 2 or a < b:
                     lines = lines + cells * vec[low, :]
-                    out[low, :] = out[low, :] + jnp.sum(moved, axis=0, keepdims=True)
+                    part[low, :] = part[low, :] + jnp.sum(moved, axis=0, keepdims=True)
                 elif a > b:
                     lines = lines + cells * vec[high, :]
-                    out[high, :] = out[high, :] + jnp.sum(moved, axis=0, keepdims=True)
+                    part[high, :] = part[high, :] + jnp.sum(moved, axis=0, keepdims=True)
                 else:
                     lines = lines + cells * jnp.where(lower, vec[low, :], vec[high, :])
-                    out[low, :] = out[low, :] + jnp.sum(jnp.where(lower, moved, 0.0), axis=0, keepdims=True)
-                    out[high, :] = out[high, :] + jnp.sum(jnp.where(lower, 0.0, moved), axis=0, keepdims=True)
-            out[here, :] = out[here, :] + to_row(jnp.sum(lines, axis=1, keepdims=True))
+                    part[low, :] = part[low, :] + jnp.sum(jnp.where(lower, moved, 0.0), axis=0, keepdims=True)
+                    part[high, :] = part[high, :] + jnp.sum(jnp.where(lower, 0.0, moved), axis=0, keepdims=True)
+            part[here, :] = part[here, :] + to_row(jnp.sum(lines, axis=1, keepdims=True))
 
     def apply_centre(e):
         ex_x[e, s] = jnp.zeros((PAD, LANES), F32)
@@ -357,12 +360,13 @@
         lax.fori_loop(0, 4, block, 0)
 
     def trade_edges(e, first=None, last=None):
-        first = ex_x.at[e, s, pl.ds(0, 8)] if first is None else first
-        last = ex_x.at[e, s, pl.ds(16, 8)] if last is None else last
+        part = pl.ds(0, EDGE)
+        first = ex_x.at[e, s, part] if first is None else first
+        last = ex_x.at[e, s, pl.ds(16, EDGE)] if last is None else last
         for i in range(RING):
-            remote(last, ex_e.at[e, s], exs_e.at[e + 1], exr_e.at[e + 1], right_edge[i])
+            remote(last, ex_e.at[e, s, part], exs_e.at[e + 1], exr_e.at[e + 1], right_edge[i])
         for i in range(RING):
-            remote(first, ex_e.at[e, RING + s], exs_e.at[e + 1], exr_e.at[e + 1], left_edge[i])
+            remote(first, ex_e.at[e, RING + s, part], exs_e.at[e + 1], exr_e.at[e + 1], left_edge[i])
 
     def trade_ring(e):
         for peer in ring_peers:
@@ -373,7 +377,7 @@
         return (ex_x[e, 0] + ex_x[e, 1]) + (ex_x[e, 2] + ex_x[e, 3])
 
     def gather_edges(e, total):
-        drain(ex_e.at[e], exr_e.at[e + 1])
+        drain(ex_e.at[e, pl.ds(0, EDGE)], exr_e.at[e + 1])
         left = (ex_e[e, 0] + ex_e[e, 1]) + (ex_e[e, 2] + ex_e[e, 3])
         right = (ex_e[e, 4] + ex_e[e, 5]) + (ex_e[e, 6] + ex_e[e, 7])
         return extend(total, left, right)
@@ -440,7 +444,6 @@
     relay(blocks - 2)
     relay(0)
     relay(blocks - 1)
-    send_direct(blocks - 2)
 
     part = gather_ring(1)
     vec[...] = scale * (outer * part + weight * image0)
@@ -450,7 +453,7 @@
     apply_sides(2)
     trade_edges(2)
     trade_ring(2)
-    for i in (0, blocks - 1):
+    for i in (blocks - 2, 0, blocks - 1):
         send_direct(i)
     for i in range(4, blocks - 2):
         send_direct(i)
@@ -529,7 +532,7 @@
     lax.fori_loop(0, 4, finish_side, 0)
     sides[0] = ld_acc[0:8, :]
     sides[1] = ld_acc[16:24, :]
-    trade_edges(3, sides.at[0], sides.at[1])
+    trade_edges(3, sides.at[0, pl.ds(0, EDGE)], sides.at[1, pl.ds(0, EDGE)])
     lax.fori_loop(2, blocks - 2, finish_centre, 0)
     ex_x[3, s] = ld_acc[...]
     trade_ring(3)
@@ -539,10 +542,10 @@
     alpha2 = rr2 / curve2
     dir2 = res2 + beta1 * dir1
     effects = alpha0 * marginal + alpha1 * dir1 + alpha2 * dir2
-    eff_out[...] = effects[2 : 2 + tiles]
+    out[0:tiles, :] = effects[2 : 2 + tiles]
 
     scores = gather_edges(3, gather_ring(3)) + diag * diag
-    ld_out[...] = scores[2 : 2 + tiles]
+    out[tiles : 2 * tiles, :] = scores[2 : 2 + tiles]
 
     drain(halo_l, halo_send.at[0])
     drain(halo_r, halo_send.at[1])
@@ -550,7 +553,7 @@
     drain(st_e, exs_e.at[0])
     for e in range(4):
         drain(ex_x.at[e, pl.ds(0, 3)], exs_x.at[e + 1])
-        drain(ex_e.at[e], exs_e.at[e + 1])
+        drain(ex_e.at[e, pl.ds(0, EDGE)], exs_e.at[e + 1])
     for r in range(3):
         drain(red.at[r, pl.ds(0, nvar - 1)], red_send.at[r])
     drain(gram.at[pl.ds(0, 3 * blocks // 4)], rs_send)
@@ -566,11 +569,11 @@
     geom = (nvar, near, far, local * RING)
     vmem = pl.BlockSpec(memory_space=pltpu.VMEM)
     dma = pltpu.SemaphoreType.DMA
-    effects, scores = pl.pallas_call(
+    both = pl.pallas_call(
         functools.partial(kernel, geom),
-        out_shape=[jax.ShapeDtypeStruct((tiles, LANES), F32)] * 2,
+        out_shape=jax.ShapeDtypeStruct((2 * tiles, LANES), F32),
         in_specs=[pl.BlockSpec(memory_space=pltpu.HBM)] * 3,
-        out_specs=[vmem, vmem],
+        out_specs=vmem,
         scratch_shapes=[
             pltpu.VMEM((local, width), F32),
             pltpu.VMEM((local, WIDE), F32),
@@ -585,9 +588,9 @@
             pltpu.VMEM((local, LANES), F32),
             pltpu.VMEM((tiles, LANES), jnp.int32),
             pltpu.VMEM((RING, 3 * PAD, LANES), F32),
-            pltpu.VMEM((32, LANES), F32),
-            pltpu.VMEM((32, LANES), F32),
-            pltpu.VMEM((2 * RING, 32, LANES), F32),
+            pltpu.VMEM((4 * EDGE, LANES), F32),
+            pltpu.VMEM((4 * EDGE, LANES), F32),
+            pltpu.VMEM((2 * RING, 4 * EDGE, LANES), F32),
             pltpu.VMEM((4, RING, PAD, LANES), F32),
             pltpu.VMEM((4, 2 * RING, 8, LANES), F32),
             pltpu.VMEM((3, nvar, 8, LANES), F32),
@@ -620,7 +623,7 @@
             collective_id=0, has_side_effects=True, vmem_limit_bytes=48 * 1024 * 1024
         ),
     )(genotypes, phenotype.reshape(chunks, LANES), win_start.reshape(tiles, LANES))
-    return effects.reshape(width), scores.reshape(width)
+    return both[:tiles].reshape(width), both[tiles:].reshape(width)
 
 
 def solution(mesh):

time: 59 us -> 57.2 us (0.969)
  Pallas kernels: 55.6 us -> 54.4 us
  local copies, waits for them, and re-layouts: 2.58 us -> 1.98 us
    unnamed x6 -> x4, local copies, waits for them, and re-layouts: 2.58 us -> 1.38 us
    pallas_call x1, Pallas kernels: 55.6 us -> 54.4 us  [shards(): pl.pallas_call(functools.partial(kernel, geom), out_shape=jax.ShapeDtypeS...]
    reshape x0 -> x1, local copies, waits for them, and re-layouts: none -> 0.61 us  [shards(): return (both[:tiles].reshape(width), both[tiles:].reshape(width))]
where the time goes in v5:
time: 57.2 us; the launch traced here: 57.1 us
  Pallas kernels  54.4 us (95%)
  local copies, waits for them, and re-layouts  1.98 us (3%)
  between operations  0.65 us (1%)
    pallas_call x1, Pallas kernels, shards(): pl.pallas_call(functools.partial(kernel, geom), out_shape=jax.ShapeDtypeS...  54.4 us
    unnamed x4, local copies, waits for them, and re-layouts  1.38 us

profile of v5, /device:TPU:0, one launch (start us, length us, event | category | flops | bytes accessed | tf_op | source)
XLA Modules:
  0.0 57.1 jit_solution(9421039384120338257)
XLA Ops:
  0.6 0.0 copy-start
  0.6 0.7 %copy-done = s32[2048]{0:T(1024)S(1)} copy-done((s32[2048]{0:T(1024)S(1)}, s32[2048]{0:T(1024)}, u32[]{:S(2)}) %copy-start) | copy-done | bytes 8216
  1.3 0.0 copy-start.1
  1.3 0.7 %copy-done.1 = f32[1024]{0:T(1024)S(1)} copy-done((f32[1024]{0:T(1024)S(1)}, f32[1024]{0:T(1024)}, u32[]{:S(2)}) %copy-start.1) | copy-done | bytes 4120
  2.0 54.4 %shard_map.50 = f32[32,128]{1,0:T(8,128)S(1)} custom-call(f32[1024,2048]{1,0:T(8,128)} %g_hbm.1, f32[8,128]{1,0:T(8,128)S(1)} %bitcast.7, s32[16,128]{1,0:T(8,128)S(1)} %bitcast.6), custom_call_target="tpu_custom_call" | custom-call | tf_op jit(solution)/shard_map/pallas_call | solution.py:572
  56.4 0.6 %slice_bitcast_fusion = (f32[2048]{0:T(1024)}, f32[2048]{0:T(1024)}) fusion(f32[32,128]{1,0:T(8,128)S(1)} %shard_map.50), kind=kLoop, calls=%fused_computation | loop fusion | bytes 32768 | tf_op jit(solution)/shard_map/reshape | solution.py:626
Async XLA Ops:
  0.6 0.7 %copy-start = (s32[2048]{0:T(1024)S(1)}, s32[2048]{0:T(1024)}, u32[]{:S(2)}) copy-start(s32[2048]{0:T(1024)} %param.6) | copy-start | bytes 24580
  1.3 0.7 %copy-start.1 = (f32[1024]{0:T(1024)S(1)}, f32[1024]{0:T(1024)}, u32[]{:S(2)}) copy-start(f32[1024]{0:T(1024)} %param.5) | copy-start | bytes 12292

commit v6 on v5

--- a/solution.py
+++ b/solution.py
@@ -370,10 +370,11 @@
 
     def trade_ring(e):
         for peer in ring_peers:
-            remote(ex_x.at[e, s], ex_x.at[e, s], exs_x.at[e + 1], exr_x.at[e + 1], peer)
+            line = ex_x.at[e, s, pl.ds(0, tiles + EDGE)]
+            remote(line, line, exs_x.at[e + 1], exr_x.at[e + 1], peer)
 
     def gather_ring(e):
-        drain(ex_x.at[e, pl.ds(0, 3)], exr_x.at[e + 1])
+        drain(ex_x.at[e, pl.ds(0, 3), pl.ds(0, tiles + EDGE)], exr_x.at[e + 1])
         return (ex_x[e, 0] + ex_x[e, 1]) + (ex_x[e, 2] + ex_x[e, 3])
 
     def gather_edges(e, total):
@@ -552,7 +553,7 @@
     drain(st_x.at[pl.ds(0, 3)], exs_x.at[0])
     drain(st_e, exs_e.at[0])
     for e in range(4):
-        drain(ex_x.at[e, pl.ds(0, 3)], exs_x.at[e + 1])
+        drain(ex_x.at[e, pl.ds(0, 3), pl.ds(0, tiles + EDGE)], exs_x.at[e + 1])
         drain(ex_e.at[e, pl.ds(0, EDGE)], exs_e.at[e + 1])
     for r in range(3):
         drain(red.at[r, pl.ds(0, nvar - 1)], red_send.at[r])

time: 57.2 us -> 57 us (level)
  no operation moved by 1% of the time
where the time goes in v6:
time: 57 us; the launch traced here: 56.8 us
  Pallas kernels  54.2 us (95%)
  local copies, waits for them, and re-layouts  1.98 us (3%)
  between operations  0.65 us (1%)
    pallas_call x1, Pallas kernels, shards(): pl.pallas_call(functools.partial(kernel, geom), out_shape=jax.ShapeDtypeS...  54.2 us
    unnamed x4, local copies, waits for them, and re-layouts  1.38 us

profile of v6, /device:TPU:0, one launch (start us, length us, event | category | flops | bytes accessed | tf_op | source)
XLA Modules:
  0.0 56.8 jit_solution(5514561457057656625)
XLA Ops:
  0.6 0.0 copy-start
  0.6 0.7 %copy-done = s32[2048]{0:T(1024)S(1)} copy-done((s32[2048]{0:T(1024)S(1)}, s32[2048]{0:T(1024)}, u32[]{:S(2)}) %copy-start) | copy-done | bytes 8216
  1.3 0.0 copy-start.1
  1.3 0.7 %copy-done.1 = f32[1024]{0:T(1024)S(1)} copy-done((f32[1024]{0:T(1024)S(1)}, f32[1024]{0:T(1024)}, u32[]{:S(2)}) %copy-start.1) | copy-done | bytes 4120
  2.0 54.2 %shard_map.50 = f32[32,128]{1,0:T(8,128)S(1)} custom-call(f32[1024,2048]{1,0:T(8,128)} %g_hbm.1, f32[8,128]{1,0:T(8,128)S(1)} %bitcast.7, s32[16,128]{1,0:T(8,128)S(1)} %bitcast.6), custom_call_target="tpu_custom_call" | custom-call | tf_op jit(solution)/shard_map/pallas_call | solution.py:573
  56.2 0.6 %slice_bitcast_fusion = (f32[2048]{0:T(1024)}, f32[2048]{0:T(1024)}) fusion(f32[32,128]{1,0:T(8,128)S(1)} %shard_map.50), kind=kLoop, calls=%fused_computation | loop fusion | bytes 32768 | tf_op jit(solution)/shard_map/reshape | solution.py:627
Async XLA Ops:
  0.6 0.7 %copy-start = (s32[2048]{0:T(1024)S(1)}, s32[2048]{0:T(1024)}, u32[]{:S(2)}) copy-start(s32[2048]{0:T(1024)} %param.6) | copy-start | bytes 24580
  1.3 0.7 %copy-start.1 = (f32[1024]{0:T(1024)S(1)}, f32[1024]{0:T(1024)}, u32[]{:S(2)}) copy-start(f32[1024]{0:T(1024)} %param.5) | copy-start | bytes 12292
